TPU v7x, 32 devices: a whole 2x2x4 slice. The times are simulated.
32 devices in a mesh: grp: 4 (over x, core), mem: 8 (over z, y).
Axes of the slice: x: 2, y: 2, z: 4, core: 2. Of those that a mesh axis runs over, the one named last changes fastest.
Arguments:
- features: bfloat16 [32768, 4096], P(('grp', 'mem')), may hold values from -0.09375 to 0.09375
- re_features: bfloat16 [32768, 256], P(('grp', 'mem')), may hold values from -6 to 6
- member_id: int32 [32768], P(('grp', 'mem')), may hold values from 0 to 255, as said below
- slot: int32 [32768], P(('grp', 'mem')), may hold values from 0 to 2047, as said below
- labels: int32 [32768], P(('grp', 'mem')), may hold values 0 or 1
- offsets: float32 [32768], P(('grp', 'mem')), may hold values from -6 to 6
- feature_scale: float32 [4096], replicated, may hold values from 0.3 to 3
- w_start: float32 [4096], replicated, may hold values from -4 to 4
Outputs:
- fixed_weights: float32 [4096], replicated
- member_coef: float32 [256, 256], P(('grp', 'mem'))
- row_offsets: float32 [32768], P(('grp', 'mem'))
Inputs may be any that keep to these rules, and one draw needn't show every extreme that they name: A row of device k (devices counted along grp, then mem) belongs to group k // 8: member_id // 64 is that group, and (member_id mod 64) // 8 equals slot // 256. Rows per member are uneven. Within one device's rows the slots are distinct; slot // 256 is the mem index that owns the row's member, so at most 256 rows of one device go to one owner, and in every group one owner receives exactly 256 rows from every device of the group.
All inputs are finite; a program needn't handle non-finite values. No bound on the sum of `labels` on one device may be relied on, other than what follows from the above.
Results may differ from a plain program's by a relative error of at most 0.0003.
Values may be sent and summed in bfloat16 or wider, within the bound.
A program may use at most 64 MiB of HBM per device.

v0:
```python
import functools

import jax
import jax.numpy as jnp
from jax import lax
from jax.experimental import pallas as pl
from jax.experimental.pallas import tpu as pltpu
from jax.sharding import PartitionSpec as P

MEM_DEV = 8
NEWTON = 2
CG_ITERS = 3
LANES = 128
BLOCK = 32

ridge_fixed = 1.0
ridge_member = 1.0
MESH_ID = pl.DeviceIdType.MESH
NT = (((1,), (1,)), ((), ()))
NN = (((1,), (0,)), ((), ()))
TN = (((0,), (0,)), ((), ()))


def pair_rows(row):
    upper = row.astype(jnp.bfloat16).astype(jnp.float32)
    lower = (row - upper).astype(jnp.bfloat16).astype(jnp.float32)
    at = lax.broadcasted_iota(jnp.int32, (16, row.shape[1]), 0)
    both = jnp.where(at == 0, upper, jnp.where(at == 1, lower, 0.0))
    return both.astype(jnp.bfloat16)


def three_parts(value):
    first = value.astype(jnp.bfloat16)
    rest = value - first.astype(jnp.float32)
    second = rest.astype(jnp.bfloat16)
    third = (rest - second.astype(jnp.float32)).astype(jnp.bfloat16)
    return first, second, third


def invert_blocks(blocks):
    lane = lax.broadcasted_iota(jnp.int32, (BLOCK, LANES), 1)
    sub = lax.broadcasted_iota(jnp.int32, (BLOCK, LANES), 0)
    base = lane // BLOCK * BLOCK
    place = lane % BLOCK
    for k in range(0, BLOCK, 2):
        one, two = place == k, place == k + 1
        new = []
        for value in blocks:
            left = jnp.take_along_axis(value, base + k, axis=1)
            right = jnp.take_along_axis(value, base + k + 1, axis=1)
            a, b = left[k : k + 1, :], right[k : k + 1, :]
            c, d = left[k + 1 : k + 2, :], right[k + 1 : k + 2, :]
            inverse = 1.0 / (a * d - b * c)
            a, b, c, d = d * inverse, -b * inverse, -c * inverse, a * inverse
            top, low = value[k : k + 1, :], value[k + 1 : k + 2, :]
            at_one, at_two = one[0:1, :], two[0:1, :]
            first = jnp.where(at_one, a, jnp.where(at_two, b, a * top + b * low))
            second = jnp.where(at_one, c, jnp.where(at_two, d, c * top + d * low))
            value = jnp.where(one | two, 0.0, value) - left * first - right * second
            value = jnp.where(sub == k, first, jnp.where(sub == k + 1, second, value))
            new.append(value)
        blocks = new
        yield blocks


def fit_members(z_ref, zt_ref, curv_row, resid_row, local, coef_ref, gram, upper, lower):
    width = z_ref.shape[1]
    slots = z_ref.shape[0]
    count = coef_ref.shape[0]
    per = LANES // BLOCK
    blocks = width // BLOCK
    weighted = zt_ref[...].astype(jnp.float32) * curv_row
    first = weighted.astype(jnp.bfloat16)
    upper[...] = first
    lower[...] = (weighted - first.astype(jnp.float32)).astype(jnp.bfloat16)
    eye = (
        lax.broadcasted_iota(jnp.int32, (width, width), 0)
        == lax.broadcasted_iota(jnp.int32, (width, width), 1)
    ).astype(jnp.float32)

    @pl.loop(0, count)
    def _(m):
        mask = jnp.where(local == m.astype(jnp.float32), 1.0, 0.0).astype(jnp.bfloat16)
        total = lax.dot_general(
            upper[...] * mask, z_ref[...], NN, preferred_element_type=jnp.float32
        ) + lax.dot_general(
            lower[...] * mask, z_ref[...], NN, preferred_element_type=jnp.float32
        )
        gram[m] = total + ridge_member * eye

    member = lax.broadcasted_iota(jnp.int32, (count, slots), 0).astype(jnp.float32)
    own = member == local
    masked = jnp.where(own, resid_row, 0.0)
    high = masked.astype(jnp.bfloat16)
    low = (masked - high.astype(jnp.float32)).astype(jnp.bfloat16)
    grad = lax.dot_general(
        high, z_ref[...], NN, preferred_element_type=jnp.float32
    ) + lax.dot_general(low, z_ref[...], NN, preferred_element_type=jnp.float32)
    rhs = [grad[m : m + 1, :] for m in range(count)]
    exact = dict(preferred_element_type=jnp.float32, precision=lax.Precision.HIGHEST)
    inverse_of = []
    heads = {}
    rows_now = [gram[m, 0:BLOCK, :] for m in range(count)]
    start = 0
    later = []

    def trailing(m, first, start, left_cat, right_cat):
        update = lax.dot_general(left_cat, right_cat, TN, preferred_element_type=jnp.float32)
        gram[m, first:width, start:width] = gram[m, first:width, start:width] - update[first - start :]

    for b in range(blocks):
        lo, hi = b * BLOCK, (b + 1) * BLOCK
        squares = [rows_now[m][:, lo - start : hi - start] for m in range(count)]
        packed = [
            jnp.concatenate(squares[at : at + per], axis=1) for at in range(0, count, per)
        ]
        for step, packed in enumerate(invert_blocks(packed)):
            if later and step % 2 == 1:
                later.pop(0)()
        while later:
            later.pop(0)()
        inverses = [
            packed[m // per][:, m % per * BLOCK : (m % per + 1) * BLOCK] for m in range(count)
        ]
        panels = []
        following = []
        new_start = hi // LANES * LANES
        for m in range(count):
            head = rhs[m][:, lo - start : hi - start]
            heads[(m, b)] = head
            if hi == width:
                continue
            right = rows_now[m][:, new_start - start :]
            panel = lax.dot_general(inverses[m], right, NN, **exact)
            panels.append(panel)
            a1, a2, a3 = three_parts(right)
            b1, b2, b3 = three_parts(panel)
            left_cat = jnp.concatenate([a1, a1, a2, a2, a1, a3], axis=0)
            right_cat = jnp.concatenate([b1, b2, b1, b2, b3, b1], axis=0)
            skip = hi - new_start
            following.append(
                gram[m, hi : hi + BLOCK, new_start:width]
                - lax.dot_general(
                    left_cat[:, skip : skip + BLOCK],
                    right_cat,
                    TN,
                    preferred_element_type=jnp.float32,
                )
            )
            if hi + BLOCK < width:
                later.append(
                    functools.partial(trailing, m, hi + BLOCK, new_start, left_cat, right_cat)
                )
            rhs[m] = rhs[m][:, new_start - start :] - lax.dot_general(head, panel, NN, **exact)
        rows_now = following
        inverse_of.append((inverses, panels, new_start))
        start = new_start
    pieces = [[None] * blocks for _ in range(count)]
    for b in reversed(range(blocks)):
        inverses, panels, begin = inverse_of[b]
        for m in range(count):
            part = lax.dot_general(heads[(m, b)], inverses[m], NN, **exact)
            if panels:
                gap = (b + 1) * BLOCK - begin
                tail = ([jnp.zeros((1, gap), jnp.float32)] if gap else []) + pieces[m][b + 1 :]
                tail = jnp.concatenate(tail, axis=1) if len(tail) > 1 else tail[0]
                part = part - lax.dot_general(tail, panels[m], NT, **exact)
            pieces[m][b] = part
    solved = [jnp.concatenate(pieces[m], axis=1) for m in range(count)]
    coef = -jnp.concatenate(solved, axis=0)
    coef_ref[...] = coef
    high = coef.astype(jnp.bfloat16)
    low = (coef - high.astype(jnp.float32)).astype(jnp.bfloat16)
    scores = lax.dot_general(
        high, zt_ref[...], NN, preferred_element_type=jnp.float32
    ) + lax.dot_general(low, zt_ref[...], NN, preferred_element_type=jnp.float32)
    return jnp.sum(jnp.where(own, scores, 0.0), axis=0, keepdims=True)


def window_kernel(
    n_grp, n_mem,
    feat_hbm, re_hbm, member_hbm, slot_hbm, label_hbm, offset_hbm, scale_hbm, start_hbm,
    weight_ref, coef_ref, offsets_ref,
    feat, re_ref, member_ref, slot_ref, label_ref, offset_ref, scale_ref, vec_w,
    vec_u, vec_r, vec_p, curv, near_send, near_recv, far_send, far_recv,
    pick, z_send, z_ref, zs_ref, zt_ref, w_send, w_recv, s_send, s_recv, gram, upper, lower, row_vals,
    load_sem, feat_sem, ns_sem, nr_sem, fs_sem, fr_sem, zs_sem, zr_sem, ws_sem, wr_sem, ss_sem, sr_sem,
):
    rows, width = feat.shape
    lines = width // LANES
    slots = z_ref.shape[0]
    cap = slots // n_mem
    calls = NEWTON * (CG_ITERS + 1)
    each = n_mem // calls
    me_grp = lax.axis_index("grp")
    me_mem = lax.axis_index("mem")

    loads = [
        pltpu.make_async_copy(source, target, load_sem.at[i])
        for i, (source, target) in enumerate(
            (
                (scale_hbm, scale_ref), (start_hbm, vec_w), (offset_hbm, offset_ref),
                (label_hbm, label_ref), (slot_hbm, slot_ref), (member_hbm, member_ref),
                (re_hbm, re_ref),
            )
        )
    ]
    feat_loads = [
        pltpu.make_async_copy(
            feat_hbm.at[pl.ds(first, 256)], feat.at[pl.ds(first, 256)], feat_sem.at[first // 256]
        )
        for first in range(0, rows, 256)
    ]
    for load in loads[:4] + feat_loads + loads[4:]:
        load.start()

    low = 2
    high = n_mem // low
    near = n_grp * low
    me_low = lax.rem(me_mem, low)
    me_high = me_mem // low
    me_near = me_grp * low + me_low

    def near_peer(turn):
        other = lax.rem(me_near + turn, near)
        return (other // low, me_high * low + lax.rem(other, low))

    def far_peer(turn):
        return (me_grp, lax.rem(me_high + turn, high) * low + me_low)

    barrier = pltpu.get_barrier_semaphore()
    for turn in range(1, n_mem):
        pl.semaphore_signal(
            barrier, inc=1, device_id=(me_grp, lax.rem(me_mem + turn, n_mem)), device_id_type=MESH_ID
        )
    for turn in range(1, near):
        pl.semaphore_signal(barrier, inc=1, device_id=near_peer(turn), device_id_type=MESH_ID)
    pl.semaphore_wait(barrier, n_mem - 1 + near - 1)
    for load in loads[:4]:
        load.wait()

    def peer(turn):
        return (me_grp, lax.rem(me_mem + turn, n_mem))

    def z_copy(turn):
        return pltpu.make_async_remote_copy(
            src_ref=z_send.at[turn - 1],
            dst_ref=z_ref.at[pl.ds(pl.multiple_of(me_mem * cap, cap), cap)],
            send_sem=zs_sem.at[turn - 1],
            recv_sem=zr_sem.at[turn - 1],
            device_id=peer(turn),
            device_id_type=MESH_ID,
        )

    def build(turn):
        first = pl.multiple_of(lax.rem(me_mem + turn, n_mem) * cap, cap)
        at = lax.broadcasted_iota(jnp.int32, (cap, rows), 0) + first
        chosen = jnp.where(at == slot_ref[...], 1.0, 0.0).astype(jnp.bfloat16)
        pick[pl.ds(first, cap), :] = chosen
        block = lax.dot_general(chosen, re_ref[...], NN, preferred_element_type=jnp.float32)
        block = block.astype(jnp.bfloat16)

        @pl.when(turn < n_mem)
        def _():
            z_send[turn - 1] = block

        @pl.when(turn == n_mem)
        def _():
            z_ref[pl.ds(pl.multiple_of(me_mem * cap, cap), cap), :] = block

    def exchange(value, call, size, me, peer_of, source, slots_of, sends, recvs, between=None):
        source[call] = value
        copies = []
        for turn in range(1, size):
            copies.append(
                pltpu.make_async_remote_copy(
                    src_ref=source.at[call],
                    dst_ref=slots_of.at[call, me],
                    send_sem=sends.at[call, turn - 1],
                    recv_sem=recvs.at[call, turn - 1],
                    device_id=peer_of(turn),
                    device_id_type=MESH_ID,
                )
            )
        for copy in copies:
            copy.start()
        slots_of[call, me] = value
        if between is not None:
            between()
        for copy in copies:
            copy.wait()
        parts = [slots_of[call, i] for i in range(size)]
        while len(parts) > 1:
            parts = [parts[i] + parts[i + 1] for i in range(0, len(parts), 2)]
        return parts[0]

    def all_sum(value, call):
        def fill():
            for q in range(each):
                build(1 + call * each + q)

        value = exchange(
            value, call, near, me_near, near_peer, near_send, near_recv, ns_sem, nr_sem, fill
        )
        value = exchange(
            value, call, high, me_high, far_peer, far_send, far_recv, fs_sem, fr_sem
        )
        for q in range(each):
            turn = 1 + call * each + q

            @pl.when(turn < n_mem)
            def _():
                z_copy(turn).start()

        return value

    def times_rows(vector, loading=None):
        row = jnp.concatenate([vector[i : i + 1, :] for i in range(lines)], axis=1)
        pair = pair_rows(row)
        parts = []
        for first in range(0, rows, 256):
            if loading is not None:
                @pl.when(loading == 0)
                def _():
                    feat_loads[first // 256].wait()
            got = lax.dot_general(
                pair, feat[first : first + 256, :], NT, preferred_element_type=jnp.float32
            )
            parts.append(got[0:1] + got[1:2])
        return jnp.concatenate(parts, axis=1)

    def times_columns(row):
        pair = pair_rows(row)
        parts = []
        for first in range(0, width, 256):
            got = lax.dot_general(
                pair, feat[:, first : first + 256], NN, preferred_element_type=jnp.float32
            )
            got = got[0:1] + got[1:2]
            parts += [got[:, at : at + LANES] for at in range(0, 256, LANES)]
        return jnp.concatenate(parts, axis=0)

    def total(value):
        return jnp.sum(jnp.sum(value, axis=1, keepdims=True), axis=0, keepdims=True)

    scale = scale_ref[...]
    target = label_ref[...].astype(jnp.float32)

    def newton(step, carry):
        base = step * (CG_ITERS + 1)
        weights = vec_w[...]
        margin = times_rows(scale * weights, step) + offset_ref[...]
        prob = 1.0 / (1.0 + jnp.exp(-margin))
        curv[...] = prob * (1.0 - prob)
        grad = times_columns(prob - target)

        @pl.when(step == 0)
        def _():
            for load in loads[4:]:
                load.wait()

        summed = all_sum(grad, base)
        resid = -(scale * summed + ridge_fixed * weights)
        vec_r[...] = resid
        vec_p[...] = resid
        vec_u[...] = jnp.zeros_like(resid)

        def cg(k, norm):
            direction = vec_p[...]
            inner = curv[...] * times_rows(scale * direction)
            image = scale * all_sum(times_columns(inner), base + 1 + k) + ridge_fixed * direction
            size = norm / total(direction * image)
            vec_u[...] = vec_u[...] + size * direction
            left = vec_r[...] - size * image
            vec_r[...] = left
            new_norm = total(left * left)
            vec_p[...] = left + new_norm / norm * direction
            return new_norm

        lax.fori_loop(0, CG_ITERS, cg, total(resid * resid))
        vec_w[...] = weights + vec_u[...]
        return carry

    lax.fori_loop(0, NEWTON, newton, 0)
    weights = vec_w[...]
    weight_ref[...] = weights
    score = times_rows(scale * weights)
    prob = 1.0 / (1.0 + jnp.exp(-score))
    local_id = lax.rem(member_ref[...], MEM_DEV).astype(jnp.float32)
    row_vals[...] = jnp.zeros_like(row_vals)
    row_vals[0:1, :] = prob * (1.0 - prob)
    row_vals[1:2, :] = prob - target
    row_vals[2:3, :] = local_id
    parts = jnp.concatenate([p.astype(jnp.float32) for p in three_parts(row_vals[...])], axis=0)
    parts = jnp.concatenate([parts, jnp.zeros_like(parts[0:8])], axis=0).astype(jnp.bfloat16)

    def small_copy(source, target, turn, sends, recvs):
        return pltpu.make_async_remote_copy(
            src_ref=source.at[turn - 1],
            dst_ref=target.at[turn - 1],
            send_sem=sends.at[turn - 1],
            recv_sem=recvs.at[turn - 1],
            device_id=peer(turn),
            device_id_type=MESH_ID,
        )

    for turn in range(1, n_mem + 1):
        first = pl.multiple_of(lax.rem(me_mem + turn, n_mem) * cap, cap)
        got = lax.dot_general(
            parts, pick[pl.ds(first, cap), :], NT, preferred_element_type=jnp.float32
        )
        got = got[0:8] + got[8:16] + got[16:24]
        if turn < n_mem:
            w_send[turn - 1] = got
            small_copy(w_send, w_recv, turn, ws_sem, wr_sem).start()
        else:
            w_recv[n_mem - 1] = got
    for turn in range(1, n_mem):
        z_copy(turn).wait()
    for turn in range(1, n_mem + 1):
        source = lax.rem(me_mem + n_mem - turn, n_mem)
        block = z_ref[pl.ds(pl.multiple_of(source * cap, cap), cap), :]
        zt_ref[:, (turn - 1) * cap : turn * cap] = block.T
        zs_ref[(turn - 1) * cap : turn * cap, :] = block
    for turn in range(1, n_mem):
        small_copy(w_send, w_recv, turn, ws_sem, wr_sem).wait()
    arrived = jnp.concatenate([w_recv[t] for t in range(n_mem)], axis=1)
    scores = fit_members(
        zs_ref, zt_ref, arrived[0:1], arrived[1:2], arrived[2:3], coef_ref, gram, upper, lower
    )
    for turn in range(1, n_mem + 1):
        back = jnp.broadcast_to(scores[:, (turn - 1) * cap : turn * cap], (8, cap))
        if turn < n_mem:
            s_send[n_mem - turn - 1] = back
        else:
            s_recv[n_mem - 1] = back
    for turn in range(1, n_mem):
        small_copy(s_send, s_recv, turn, ss_sem, sr_sem).start()
    for turn in range(1, n_mem):
        small_copy(s_send, s_recv, turn, ss_sem, sr_sem).wait()
    result = jnp.zeros((1, rows), jnp.float32)
    for turn in range(1, n_mem + 1):
        owner = lax.rem(me_mem + n_mem - turn, n_mem)
        value = s_recv[turn - 1][0:1]
        p1, p2, p3 = (p.astype(jnp.float32) for p in three_parts(value))
        at = lax.broadcasted_iota(jnp.int32, (16, cap), 0)
        stack = jnp.where(at == 0, p1, jnp.where(at == 1, p2, jnp.where(at == 2, p3, 0.0)))
        got = lax.dot_general(
            stack.astype(jnp.bfloat16),
            pick[pl.ds(pl.multiple_of(owner * cap, cap), cap), :],
            NN,
            preferred_element_type=jnp.float32,
        )
        result = result + (got[0:1] + got[1:2] + got[2:3])
    offsets_ref[...] = result


def on_device(n_grp, n_mem, features, re_features, member_id, slot, labels, offsets, feature_scale, w_start):
    rows, width = features.shape
    inner = re_features.shape[1]
    lines = width // LANES
    slots = 2 * rows
    cap = slots // n_mem
    near, high = 2 * n_grp, n_mem // 2
    calls = NEWTON * (CG_ITERS + 1)
    f32, bf16, i32 = jnp.float32, jnp.bfloat16, jnp.int32
    held = pltpu.VMEM((lines, LANES), f32)
    dma = pltpu.SemaphoreType.DMA
    whole = pl.BlockSpec(memory_space=pltpu.VMEM)
    weights, member_coef, row_offsets = pl.pallas_call(
        functools.partial(window_kernel, n_grp, n_mem),
        out_shape=(
            jax.ShapeDtypeStruct((lines, LANES), f32),
            jax.ShapeDtypeStruct((MEM_DEV, inner), f32),
            jax.ShapeDtypeStruct((1, rows), f32),
        ),
        in_specs=[pl.BlockSpec(memory_space=pl.ANY)] * 8,
        out_specs=(whole,) * 3,
        scratch_shapes=[
            pltpu.VMEM((rows, width), bf16),
            pltpu.VMEM((rows, inner), bf16),
            pltpu.VMEM((1, rows), i32),
            pltpu.VMEM((1, rows), i32),
            pltpu.VMEM((1, rows), i32),
            pltpu.VMEM((1, rows), f32),
            held, held, held, held, held,
            pltpu.VMEM((1, rows), f32),
            pltpu.VMEM((calls, lines, LANES), f32),
            pltpu.VMEM((calls, near, lines, LANES), f32),
            pltpu.VMEM((calls, lines, LANES), f32),
            pltpu.VMEM((calls, high, lines, LANES), f32),
            pltpu.VMEM((slots, rows), bf16),
            pltpu.VMEM((n_mem - 1, cap, inner), bf16),
            pltpu.VMEM((slots, inner), bf16),
            pltpu.VMEM((slots, inner), bf16),
            pltpu.VMEM((inner, slots), bf16),
            pltpu.VMEM((n_mem - 1, 8, cap), f32),
            pltpu.VMEM((n_mem, 8, cap), f32),
            pltpu.VMEM((n_mem - 1, 8, cap), f32),
            pltpu.VMEM((n_mem, 8, cap), f32),
            pltpu.VMEM((MEM_DEV, inner, inner), f32),
            pltpu.VMEM((inner, slots), bf16),
            pltpu.VMEM((inner, slots), bf16),
            pltpu.VMEM((8, rows), f32),
            dma((7,)),
            dma((rows // 256,)),
            dma((calls, near - 1)),
            dma((calls, near - 1)),
            dma((calls, high - 1)),
            dma((calls, high - 1)),
            dma((n_mem - 1,)),
            dma((n_mem - 1,)),
            dma((n_mem - 1,)),
            dma((n_mem - 1,)),
            dma((n_mem - 1,)),
            dma((n_mem - 1,)),
        ],
        compiler_params=pltpu.CompilerParams(
            collective_id=0, has_side_effects=True, vmem_limit_bytes=60 << 20
        ),
        name="window",
    )(
        features,
        re_features,
        member_id.reshape(1, rows),
        slot.reshape(1, rows),
        labels.reshape(1, rows),
        offsets.reshape(1, rows),
        feature_scale.reshape(lines, LANES),
        w_start.reshape(lines, LANES),
    )
    return (weights.reshape(-1), member_coef, row_offsets.reshape(-1))


def solution(mesh):
    placed = (
        P(("grp", "mem"), None),
        P(("grp", "mem"), None),
        P(("grp", "mem")),
        P(("grp", "mem")),
        P(("grp", "mem")),
        P(("grp", "mem")),
        P(),
        P(),
    )
    return jax.shard_map(
        functools.partial(on_device, mesh.shape["grp"], mesh.shape["mem"]),
        mesh=mesh,
        in_specs=placed,
        out_specs=(P(), P(("grp", "mem"), None), P(("grp", "mem"))),
        check_vma=False,
    )
```

profile of v0, /device:TPU:0, one launch (start us, length us, event | category | flops | bytes accessed | tf_op | source)
XLA Modules:
  0.0 156.2 jit_solution(8666760617349105828)
XLA Ops:
  0.6 151.7 %window.1 = (f32[32,128]{1,0:T(8,128)}, f32[8,256]{1,0:T(8,128)}, f32[1,1024]{1,0:T(1,128)}) custom-call(bf16[1024,4096]{1,0:T(8,128)(2,1)} %feat_hbm.1, bf16[1024,256]{1,0:T(8,128)(2,1)} %re_hbm.1, s32[1,1024]{1,0:T(1,128)} %bitcast.11, s32[1,1024]{1,0:T(1,128)} %bitcast.12, s32[1,1024]{1,0:T(1,128)} %bitcast.13, f32[1,1024]{1,0:T(1,128)} %bitcast.14, ...), custom_call_target="tpu_custom_call" | custom-call | tf_op jit(solution)/shard_map/window/pallas_call | solution.py:470
  152.3 1.3 copy.14
  153.7 1.3 copy.15
  155.0 1.3 copy.16
where the time goes:
time: 157 us; the launch traced here: 156 us
  Pallas kernels  152 us (97%)
  local copies, waits for them, and re-layouts  3.89 us (2%)
    pallas_call x1, Pallas kernels, on_device(): pl.pallas_call(functools.partial(window_kernel, n_grp, n_mem), out_shape=...  152 us
    unnamed x3, local copies, waits for them, and re-layouts  3.89 us

commit v1 on v0

--- a/solution.py
+++ b/solution.py
@@ -182,9 +182,9 @@
     feat_hbm, re_hbm, member_hbm, slot_hbm, label_hbm, offset_hbm, scale_hbm, start_hbm,
     weight_ref, coef_ref, offsets_ref,
     feat, re_ref, member_ref, slot_ref, label_ref, offset_ref, scale_ref, vec_w,
-    vec_u, vec_r, vec_p, curv, near_send, near_recv, far_send, far_recv,
+    vec_u, vec_r, vec_p, curv, score, near_send, near_recv, far_send, far_recv, one_send, one_recv,
     pick, z_send, z_ref, zs_ref, zt_ref, w_send, w_recv, s_send, s_recv, gram, upper, lower, row_vals,
-    load_sem, feat_sem, ns_sem, nr_sem, fs_sem, fr_sem, zs_sem, zr_sem, ws_sem, wr_sem, ss_sem, sr_sem,
+    load_sem, feat_sem, ns_sem, nr_sem, fs_sem, fr_sem, os_sem, or_sem, zs_sem, zr_sem, ws_sem, wr_sem, ss_sem, sr_sem,
 ):
     rows, width = feat.shape
     lines = width // LANES
@@ -192,6 +192,7 @@
     cap = slots // n_mem
     calls = NEWTON * (CG_ITERS + 1)
     each = n_mem // calls
+    direct = n_grp * n_mem <= 32
     me_grp = lax.axis_index("grp")
     me_mem = lax.axis_index("mem")
 
@@ -228,14 +229,25 @@
     def far_peer(turn):
         return (me_grp, lax.rem(me_high + turn, high) * low + me_low)
 
+    me_all = me_grp * n_mem + me_mem
+
+    def any_peer(turn):
+        other = lax.rem(me_all + turn, n_grp * n_mem)
+        return (other // n_mem, lax.rem(other, n_mem))
+
     barrier = pltpu.get_barrier_semaphore()
-    for turn in range(1, n_mem):
-        pl.semaphore_signal(
-            barrier, inc=1, device_id=(me_grp, lax.rem(me_mem + turn, n_mem)), device_id_type=MESH_ID
-        )
-    for turn in range(1, near):
-        pl.semaphore_signal(barrier, inc=1, device_id=near_peer(turn), device_id_type=MESH_ID)
-    pl.semaphore_wait(barrier, n_mem - 1 + near - 1)
+    if direct:
+        for turn in range(1, n_grp * n_mem):
+            pl.semaphore_signal(barrier, inc=1, device_id=any_peer(turn), device_id_type=MESH_ID)
+        pl.semaphore_wait(barrier, n_grp * n_mem - 1)
+    else:
+        for turn in range(1, n_mem):
+            pl.semaphore_signal(
+                barrier, inc=1, device_id=(me_grp, lax.rem(me_mem + turn, n_mem)), device_id_type=MESH_ID
+            )
+        for turn in range(1, near):
+            pl.semaphore_signal(barrier, inc=1, device_id=near_peer(turn), device_id_type=MESH_ID)
+        pl.semaphore_wait(barrier, n_mem - 1 + near - 1)
     for load in loads[:4]:
         load.wait()
 
@@ -270,41 +282,31 @@
 
     def exchange(value, call, size, me, peer_of, source, slots_of, sends, recvs, between=None):
         source[call] = value
-        copies = []
         for turn in range(1, size):
-            copies.append(
-                pltpu.make_async_remote_copy(
-                    src_ref=source.at[call],
-                    dst_ref=slots_of.at[call, me],
-                    send_sem=sends.at[call, turn - 1],
-                    recv_sem=recvs.at[call, turn - 1],
-                    device_id=peer_of(turn),
-                    device_id_type=MESH_ID,
-                )
-            )
-        for copy in copies:
-            copy.start()
+            pltpu.make_async_remote_copy(
+                src_ref=source.at[call],
+                dst_ref=slots_of.at[call, me],
+                send_sem=sends.at[call],
+                recv_sem=recvs.at[call],
+                device_id=peer_of(turn),
+                device_id_type=MESH_ID,
+            ).start()
         slots_of[call, me] = value
         if between is not None:
             between()
-        for copy in copies:
-            copy.wait()
+        others = slots_of.at[call, pl.ds(0, size - 1)]
+        pltpu.make_async_copy(others, others, recvs.at[call]).wait()
+        pltpu.make_async_copy(others, others, sends.at[call]).wait()
         parts = [slots_of[call, i] for i in range(size)]
         while len(parts) > 1:
             parts = [parts[i] + parts[i + 1] for i in range(0, len(parts), 2)]
         return parts[0]
 
-    def all_sum(value, call):
-        def fill():
-            for q in range(each):
-                build(1 + call * each + q)
-
-        value = exchange(
-            value, call, near, me_near, near_peer, near_send, near_recv, ns_sem, nr_sem, fill
-        )
-        value = exchange(
-            value, call, high, me_high, far_peer, far_send, far_recv, fs_sem, fr_sem
-        )
+    def regroup(call):
+        for q in range(each):
+            build(1 + call * each + q)
+
+    def forward(call):
         for q in range(each):
             turn = 1 + call * each + q
 
@@ -312,17 +314,36 @@
             def _():
                 z_copy(turn).start()
 
+    def all_sum(value, call, fill):
+        value = exchange(
+            value, call, near, me_near, near_peer, near_send, near_recv, ns_sem, nr_sem,
+            functools.partial(regroup, fill),
+        )
+        value = exchange(
+            value, call, high, me_high, far_peer, far_send, far_recv, fs_sem, fr_sem
+        )
+        forward(fill)
         return value
 
-    def times_rows(vector, loading=None):
+    def small_sum(value, call, fill):
+        value = jnp.broadcast_to(value, (1, LANES))
+        if direct:
+            value = exchange(
+                value, call, n_grp * n_mem, me_all, any_peer, one_send, one_recv, os_sem, or_sem,
+                functools.partial(regroup, fill),
+            )
+            forward(fill)
+            return value[:, 0:1]
+        wide = jnp.broadcast_to(value, (lines, LANES))
+        return all_sum(wide, NEWTON * CG_ITERS + call, fill)[0:1, 0:1]
+
+    def times_rows(vector, loading=False):
         row = jnp.concatenate([vector[i : i + 1, :] for i in range(lines)], axis=1)
         pair = pair_rows(row)
         parts = []
         for first in range(0, rows, 256):
-            if loading is not None:
-                @pl.when(loading == 0)
-                def _():
-                    feat_loads[first // 256].wait()
+            if loading:
+                feat_loads[first // 256].wait()
             got = lax.dot_general(
                 pair, feat[first : first + 256, :], NT, preferred_element_type=jnp.float32
             )
@@ -346,10 +367,11 @@
     scale = scale_ref[...]
     target = label_ref[...].astype(jnp.float32)
 
+    score[...] = times_rows(scale * vec_w[...], True)
+
     def newton(step, carry):
-        base = step * (CG_ITERS + 1)
         weights = vec_w[...]
-        margin = times_rows(scale * weights, step) + offset_ref[...]
+        margin = score[...] + offset_ref[...]
         prob = 1.0 / (1.0 + jnp.exp(-margin))
         curv[...] = prob * (1.0 - prob)
         grad = times_columns(prob - target)
@@ -359,33 +381,39 @@
             for load in loads[4:]:
                 load.wait()
 
-        summed = all_sum(grad, base)
-        resid = -(scale * summed + ridge_fixed * weights)
+        base = step * CG_ITERS
+        fill = step * (CG_ITERS + 1)
+        resid = -(scale * all_sum(grad, base, fill) + ridge_fixed * weights)
         vec_r[...] = resid
         vec_p[...] = resid
         vec_u[...] = jnp.zeros_like(resid)
 
         def cg(k, norm):
             direction = vec_p[...]
-            inner = curv[...] * times_rows(scale * direction)
-            image = scale * all_sum(times_columns(inner), base + 1 + k) + ridge_fixed * direction
+            along = times_rows(scale * direction)
+            image = all_sum(times_columns(curv[...] * along), base + 1 + k, fill + 1 + k)
+            image = scale * image + ridge_fixed * direction
             size = norm / total(direction * image)
             vec_u[...] = vec_u[...] + size * direction
+            score[...] = score[...] + size * along
             left = vec_r[...] - size * image
             vec_r[...] = left
             new_norm = total(left * left)
             vec_p[...] = left + new_norm / norm * direction
             return new_norm
 
-        lax.fori_loop(0, CG_ITERS, cg, total(resid * resid))
-        vec_w[...] = weights + vec_u[...]
+        norm = lax.fori_loop(0, CG_ITERS - 1, cg, total(resid * resid))
+        direction = vec_p[...]
+        along = times_rows(scale * direction)
+        bend = small_sum(total(curv[...] * along * along), step, fill + CG_ITERS)
+        size = norm / (bend + ridge_fixed * total(direction * direction))
+        score[...] = score[...] + size * along
+        vec_w[...] = weights + (vec_u[...] + size * direction)
         return carry
 
     lax.fori_loop(0, NEWTON, newton, 0)
-    weights = vec_w[...]
-    weight_ref[...] = weights
-    score = times_rows(scale * weights)
-    prob = 1.0 / (1.0 + jnp.exp(-score))
+    weight_ref[...] = vec_w[...]
+    prob = 1.0 / (1.0 + jnp.exp(-score[...]))
     local_id = lax.rem(member_ref[...], MEM_DEV).astype(jnp.float32)
     row_vals[...] = jnp.zeros_like(row_vals)
     row_vals[0:1, :] = prob * (1.0 - prob)
@@ -462,7 +490,9 @@
     slots = 2 * rows
     cap = slots // n_mem
     near, high = 2 * n_grp, n_mem // 2
-    calls = NEWTON * (CG_ITERS + 1)
+    direct = n_grp * n_mem <= 32
+    calls = NEWTON * CG_ITERS if direct else NEWTON * (CG_ITERS + 1)
+    every = n_grp * n_mem if direct else 2
     f32, bf16, i32 = jnp.float32, jnp.bfloat16, jnp.int32
     held = pltpu.VMEM((lines, LANES), f32)
     dma = pltpu.SemaphoreType.DMA
@@ -485,10 +515,13 @@
             pltpu.VMEM((1, rows), f32),
             held, held, held, held, held,
             pltpu.VMEM((1, rows), f32),
+            pltpu.VMEM((1, rows), f32),
             pltpu.VMEM((calls, lines, LANES), f32),
             pltpu.VMEM((calls, near, lines, LANES), f32),
             pltpu.VMEM((calls, lines, LANES), f32),
             pltpu.VMEM((calls, high, lines, LANES), f32),
+            pltpu.VMEM((NEWTON, 1, LANES), f32),
+            pltpu.VMEM((NEWTON, every, 1, LANES), f32),
             pltpu.VMEM((slots, rows), bf16),
             pltpu.VMEM((n_mem - 1, cap, inner), bf16),
             pltpu.VMEM((slots, inner), bf16),
@@ -504,10 +537,12 @@
             pltpu.VMEM((8, rows), f32),
             dma((7,)),
             dma((rows // 256,)),
-            dma((calls, near - 1)),
-            dma((calls, near - 1)),
-            dma((calls, high - 1)),
-            dma((calls, high - 1)),
+            dma((calls,)),
+            dma((calls,)),
+            dma((calls,)),
+            dma((calls,)),
+            dma((NEWTON,)),
+            dma((NEWTON,)),
             dma((n_mem - 1,)),
             dma((n_mem - 1,)),
             dma((n_mem - 1,)),

time: 157 us -> 142 us (0.904)
  Pallas kernels: 152 us -> 137 us
    pallas_call x1, Pallas kernels: 152 us -> 137 us  [on_device(): pl.pallas_call(functools.partial(window_kernel, n_grp, n_mem), out_shape=...]
where the time goes in v1:
time: 142 us
  Pallas kernels  137 us (96%)
  local copies, waits for them, and re-layouts  3.89 us (3%)
    pallas_call x1, Pallas kernels, on_device(): pl.pallas_call(functools.partial(window_kernel, n_grp, n_mem), out_shape=...  137 us
    unnamed x3, local copies, waits for them, and re-layouts  3.89 us

profile of v1, /device:TPU:0, one launch (start us, length us, event | category | flops | bytes accessed | tf_op | source)
XLA Modules:
  0.0 142.0 jit_solution(602861522890327158)
XLA Ops:
  0.6 137.4 %window.1 = (f32[32,128]{1,0:T(8,128)}, f32[8,256]{1,0:T(8,128)}, f32[1,1024]{1,0:T(1,128)}) custom-call(bf16[1024,4096]{1,0:T(8,128)(2,1)} %feat_hbm.1, bf16[1024,256]{1,0:T(8,128)(2,1)} %re_hbm.1, s32[1,1024]{1,0:T(1,128)} %bitcast.11, s32[1,1024]{1,0:T(1,128)} %bitcast.12, s32[1,1024]{1,0:T(1,128)} %bitcast.13, f32[1,1024]{1,0:T(1,128)} %bitcast.14, ...), custom_call_target="tpu_custom_call" | custom-call | tf_op jit(solution)/shard_map/window/pallas_call | solution.py:500
  138.1 1.3 copy.14
  139.4 1.3 copy.15
  140.7 1.3 copy.16

commit v2 on v1

--- a/solution.py
+++ b/solution.py
@@ -12,6 +12,7 @@
 CG_ITERS = 3
 LANES = 128
 BLOCK = 32
+BUILD_CALLS = 4
 
 ridge_fixed = 1.0
 ridge_member = 1.0
@@ -37,36 +38,55 @@
     return first, second, third
 
 
+def split_six(value, axis, left):
+    first, second, third = three_parts(value)
+    if left:
+        return jnp.concatenate([first, first, second, second, first, third], axis=axis)
+    return jnp.concatenate([first, second, first, second, third, first], axis=axis)
+
+
 def invert_blocks(blocks):
     lane = lax.broadcasted_iota(jnp.int32, (BLOCK, LANES), 1)
     sub = lax.broadcasted_iota(jnp.int32, (BLOCK, LANES), 0)
     base = lane // BLOCK * BLOCK
     place = lane % BLOCK
+
+    def column(value, k):
+        return jnp.take_along_axis(value, base + k, axis=1)
+
+    blocks = [(value, column(value, 0), column(value, 1)) for value in blocks]
     for k in range(0, BLOCK, 2):
         one, two = place == k, place == k + 1
+        at_one, at_two = one[0:1, :], two[0:1, :]
         new = []
-        for value in blocks:
-            left = jnp.take_along_axis(value, base + k, axis=1)
-            right = jnp.take_along_axis(value, base + k + 1, axis=1)
+        for value, left, right in blocks:
+            ahead = [column(value, k + 2), column(value, k + 3)] if k + 2 < BLOCK else []
             a, b = left[k : k + 1, :], right[k : k + 1, :]
             c, d = left[k + 1 : k + 2, :], right[k + 1 : k + 2, :]
             inverse = 1.0 / (a * d - b * c)
             a, b, c, d = d * inverse, -b * inverse, -c * inverse, a * inverse
+
+            def update(value, first, second):
+                value = value - left * first - right * second
+                return jnp.where(sub == k, first, jnp.where(sub == k + 1, second, value))
+
+            following = []
+            for col in ahead:
+                top, low = col[k : k + 1, :], col[k + 1 : k + 2, :]
+                following.append(update(col, a * top + b * low, c * top + d * low))
             top, low = value[k : k + 1, :], value[k + 1 : k + 2, :]
-            at_one, at_two = one[0:1, :], two[0:1, :]
             first = jnp.where(at_one, a, jnp.where(at_two, b, a * top + b * low))
             second = jnp.where(at_one, c, jnp.where(at_two, d, c * top + d * low))
-            value = jnp.where(one | two, 0.0, value) - left * first - right * second
-            value = jnp.where(sub == k, first, jnp.where(sub == k + 1, second, value))
-            new.append(value)
+            value = update(jnp.where(one | two, 0.0, value), first, second)
+            new.append((value, *(following or (left, right))))
         blocks = new
-        yield blocks
-
-
-def fit_members(z_ref, zt_ref, curv_row, resid_row, local, coef_ref, gram, upper, lower):
+        yield [value for value, _, _ in blocks]
+
+
+def fit_members(z_ref, zt_ref, curv_row, resid_row, local, gram, upper, lower):
     width = z_ref.shape[1]
     slots = z_ref.shape[0]
-    count = coef_ref.shape[0]
+    count = MEM_DEV
     per = LANES // BLOCK
     blocks = width // BLOCK
     weighted = zt_ref[...].astype(jnp.float32) * curv_row
@@ -89,92 +109,75 @@
         gram[m] = total + ridge_member * eye
 
     member = lax.broadcasted_iota(jnp.int32, (count, slots), 0).astype(jnp.float32)
-    own = member == local
-    masked = jnp.where(own, resid_row, 0.0)
+    masked = jnp.where(member == local, resid_row, 0.0)
     high = masked.astype(jnp.bfloat16)
     low = (masked - high.astype(jnp.float32)).astype(jnp.bfloat16)
-    grad = lax.dot_general(
+    goal = lax.dot_general(
         high, z_ref[...], NN, preferred_element_type=jnp.float32
     ) + lax.dot_general(low, z_ref[...], NN, preferred_element_type=jnp.float32)
-    rhs = [grad[m : m + 1, :] for m in range(count)]
-    exact = dict(preferred_element_type=jnp.float32, precision=lax.Precision.HIGHEST)
-    inverse_of = []
-    heads = {}
+
+    place = lax.broadcasted_iota(jnp.int32, (1, width), 1)
+    turn = lax.broadcasted_iota(jnp.int32, (count, width), 0)
+    lane = lax.broadcasted_iota(jnp.int32, (BLOCK, LANES), 1)
+    unit = lax.broadcasted_iota(jnp.int32, (BLOCK, width), 1)
+    unit = unit - lax.broadcasted_iota(jnp.int32, (BLOCK, width), 0)
+    later = []
+
+    def trailing(m, first, inside, left, right):
+        update = lax.dot_general(left, right, TN, preferred_element_type=jnp.float32)
+        gram[m, first:width, :] = jnp.where(inside, 0.0, gram[m, first:width, :]) - update
+
     rows_now = [gram[m, 0:BLOCK, :] for m in range(count)]
-    start = 0
-    later = []
-
-    def trailing(m, first, start, left_cat, right_cat):
-        update = lax.dot_general(left_cat, right_cat, TN, preferred_element_type=jnp.float32)
-        gram[m, first:width, start:width] = gram[m, first:width, start:width] - update[first - start :]
-
     for b in range(blocks):
         lo, hi = b * BLOCK, (b + 1) * BLOCK
-        squares = [rows_now[m][:, lo - start : hi - start] for m in range(count)]
         packed = [
-            jnp.concatenate(squares[at : at + per], axis=1) for at in range(0, count, per)
+            jnp.concatenate([rows_now[m][:, lo:hi] for m in range(at, at + per)], axis=1)
+            for at in range(0, count, per)
         ]
         for step, packed in enumerate(invert_blocks(packed)):
             if later and step % 2 == 1:
                 later.pop(0)()
         while later:
             later.pop(0)()
-        inverses = [
-            packed[m // per][:, m % per * BLOCK : (m % per + 1) * BLOCK] for m in range(count)
-        ]
+        inside = (place >= lo) & (place < hi)
         panels = []
+        for index, value in enumerate(packed):
+            left = jnp.concatenate(
+                [jnp.where(lane // BLOCK == i, value, 0.0) for i in range(per)], axis=0
+            )
+            right = jnp.concatenate(
+                [
+                    jnp.where(inside, jnp.where(unit == lo, -1.0, 0.0), rows_now[index * per + i])
+                    for i in range(per)
+                ],
+                axis=0,
+            )
+            got = lax.dot_general(
+                split_six(left, 1, True), split_six(right, 0, False), NN,
+                preferred_element_type=jnp.float32,
+            )
+            panels += [got[i * BLOCK : (i + 1) * BLOCK, :] for i in range(per)]
+        heads = split_six(goal[:, lo:hi], 1, True)
+        goal = jnp.where(inside, 0.0, goal)
         following = []
-        new_start = hi // LANES * LANES
         for m in range(count):
-            head = rhs[m][:, lo - start : hi - start]
-            heads[(m, b)] = head
-            if hi == width:
-                continue
-            right = rows_now[m][:, new_start - start :]
-            panel = lax.dot_general(inverses[m], right, NN, **exact)
-            panels.append(panel)
-            a1, a2, a3 = three_parts(right)
-            b1, b2, b3 = three_parts(panel)
-            left_cat = jnp.concatenate([a1, a1, a2, a2, a1, a3], axis=0)
-            right_cat = jnp.concatenate([b1, b2, b1, b2, b3, b1], axis=0)
-            skip = hi - new_start
-            following.append(
-                gram[m, hi : hi + BLOCK, new_start:width]
-                - lax.dot_general(
-                    left_cat[:, skip : skip + BLOCK],
-                    right_cat,
-                    TN,
-                    preferred_element_type=jnp.float32,
+            right = split_six(panels[m], 0, False)
+            if hi < width:
+                left = split_six(rows_now[m][:, hi:], 0, True)
+                update = lax.dot_general(
+                    left[:, 0:BLOCK], right, TN, preferred_element_type=jnp.float32
                 )
-            )
-            if hi + BLOCK < width:
-                later.append(
-                    functools.partial(trailing, m, hi + BLOCK, new_start, left_cat, right_cat)
-                )
-            rhs[m] = rhs[m][:, new_start - start :] - lax.dot_general(head, panel, NN, **exact)
+                following.append(jnp.where(inside, 0.0, gram[m, hi : hi + BLOCK, :]) - update)
+                if hi + BLOCK < width:
+                    later.append(
+                        functools.partial(
+                            trailing, m, hi + BLOCK, inside, left[:, BLOCK:], right
+                        )
+                    )
+            update = lax.dot_general(heads, right, NN, preferred_element_type=jnp.float32)
+            goal = goal - jnp.where(turn == m, update, 0.0)
         rows_now = following
-        inverse_of.append((inverses, panels, new_start))
-        start = new_start
-    pieces = [[None] * blocks for _ in range(count)]
-    for b in reversed(range(blocks)):
-        inverses, panels, begin = inverse_of[b]
-        for m in range(count):
-            part = lax.dot_general(heads[(m, b)], inverses[m], NN, **exact)
-            if panels:
-                gap = (b + 1) * BLOCK - begin
-                tail = ([jnp.zeros((1, gap), jnp.float32)] if gap else []) + pieces[m][b + 1 :]
-                tail = jnp.concatenate(tail, axis=1) if len(tail) > 1 else tail[0]
-                part = part - lax.dot_general(tail, panels[m], NT, **exact)
-            pieces[m][b] = part
-    solved = [jnp.concatenate(pieces[m], axis=1) for m in range(count)]
-    coef = -jnp.concatenate(solved, axis=0)
-    coef_ref[...] = coef
-    high = coef.astype(jnp.bfloat16)
-    low = (coef - high.astype(jnp.float32)).astype(jnp.bfloat16)
-    scores = lax.dot_general(
-        high, zt_ref[...], NN, preferred_element_type=jnp.float32
-    ) + lax.dot_general(low, zt_ref[...], NN, preferred_element_type=jnp.float32)
-    return jnp.sum(jnp.where(own, scores, 0.0), axis=0, keepdims=True)
+    return -goal
 
 
 def window_kernel(
@@ -183,15 +186,14 @@
     weight_ref, coef_ref, offsets_ref,
     feat, re_ref, member_ref, slot_ref, label_ref, offset_ref, scale_ref, vec_w,
     vec_u, vec_r, vec_p, curv, score, near_send, near_recv, far_send, far_recv, one_send, one_recv,
-    pick, z_send, z_ref, zs_ref, zt_ref, w_send, w_recv, s_send, s_recv, gram, upper, lower, row_vals,
-    load_sem, feat_sem, ns_sem, nr_sem, fs_sem, fr_sem, os_sem, or_sem, zs_sem, zr_sem, ws_sem, wr_sem, ss_sem, sr_sem,
+    pick, z_send, z_ref, zt_ref, w_send, w_recv, c_recv, gram, upper, lower, row_vals,
+    load_sem, feat_sem, ns_sem, nr_sem, fs_sem, fr_sem, os_sem, or_sem, zs_sem, zr_sem, ws_sem, wr_sem, cs_sem, cr_sem,
 ):
     rows, width = feat.shape
     lines = width // LANES
     slots = z_ref.shape[0]
     cap = slots // n_mem
-    calls = NEWTON * (CG_ITERS + 1)
-    each = n_mem // calls
+    each = pl.cdiv(n_mem, BUILD_CALLS)
     direct = n_grp * n_mem <= 32
     me_grp = lax.axis_index("grp")
     me_mem = lax.axis_index("mem")
@@ -257,7 +259,7 @@
     def z_copy(turn):
         return pltpu.make_async_remote_copy(
             src_ref=z_send.at[turn - 1],
-            dst_ref=z_ref.at[pl.ds(pl.multiple_of(me_mem * cap, cap), cap)],
+            dst_ref=z_ref.at[pl.ds(pl.multiple_of((turn - 1) * cap, cap), cap)],
             send_sem=zs_sem.at[turn - 1],
             recv_sem=zr_sem.at[turn - 1],
             device_id=peer(turn),
@@ -278,7 +280,7 @@
 
         @pl.when(turn == n_mem)
         def _():
-            z_ref[pl.ds(pl.multiple_of(me_mem * cap, cap), cap), :] = block
+            z_ref[(n_mem - 1) * cap :, :] = block
 
     def exchange(value, call, size, me, peer_of, source, slots_of, sends, recvs, between=None):
         source[call] = value
@@ -304,38 +306,57 @@
 
     def regroup(call):
         for q in range(each):
-            build(1 + call * each + q)
+            @pl.when(call * each + q < n_mem)
+            def _():
+                build(call * each + q + 1)
 
     def forward(call):
         for q in range(each):
-            turn = 1 + call * each + q
+            turn = call * each + q + 1
 
             @pl.when(turn < n_mem)
             def _():
                 z_copy(turn).start()
 
-    def all_sum(value, call, fill):
+    def turn_over(call):
+        for q in range(each):
+            turn = (call - 2) * each + q + 1
+
+            @pl.when((turn >= 1) & (turn < n_mem))
+            def _():
+                z_copy(turn).wait()
+
+            if cap % LANES == 0:
+
+                @pl.when((turn >= 1) & (turn <= n_mem))
+                def _():
+                    at = pl.ds(pl.multiple_of((turn - 1) * cap, cap), cap)
+                    zt_ref[:, at] = z_ref[at, :].T
+
+    def all_sum(value, call, fills=True):
         value = exchange(
             value, call, near, me_near, near_peer, near_send, near_recv, ns_sem, nr_sem,
-            functools.partial(regroup, fill),
+            functools.partial(regroup, call) if fills else None,
         )
         value = exchange(
-            value, call, high, me_high, far_peer, far_send, far_recv, fs_sem, fr_sem
+            value, call, high, me_high, far_peer, far_send, far_recv, fs_sem, fr_sem,
+            functools.partial(turn_over, call) if fills else None,
         )
-        forward(fill)
+        if fills:
+            forward(call)
         return value
 
-    def small_sum(value, call, fill):
+    def small_sum(value, call, between):
         value = jnp.broadcast_to(value, (1, LANES))
         if direct:
             value = exchange(
                 value, call, n_grp * n_mem, me_all, any_peer, one_send, one_recv, os_sem, or_sem,
-                functools.partial(regroup, fill),
-            )
-            forward(fill)
+                between,
+            )
             return value[:, 0:1]
+        between()
         wide = jnp.broadcast_to(value, (lines, LANES))
-        return all_sum(wide, NEWTON * CG_ITERS + call, fill)[0:1, 0:1]
+        return all_sum(wide, NEWTON * CG_ITERS + call, False)[0:1, 0:1]
 
     def times_rows(vector, loading=False):
         row = jnp.concatenate([vector[i : i + 1, :] for i in range(lines)], axis=1)
@@ -382,8 +403,7 @@
                 load.wait()
 
         base = step * CG_ITERS
-        fill = step * (CG_ITERS + 1)
-        resid = -(scale * all_sum(grad, base, fill) + ridge_fixed * weights)
+        resid = -(scale * all_sum(grad, base) + ridge_fixed * weights)
         vec_r[...] = resid
         vec_p[...] = resid
         vec_u[...] = jnp.zeros_like(resid)
@@ -391,7 +411,7 @@
         def cg(k, norm):
             direction = vec_p[...]
             along = times_rows(scale * direction)
-            image = all_sum(times_columns(curv[...] * along), base + 1 + k, fill + 1 + k)
+            image = all_sum(times_columns(curv[...] * along), base + 1 + k)
             image = scale * image + ridge_fixed * direction
             size = norm / total(direction * image)
             vec_u[...] = vec_u[...] + size * direction
@@ -405,82 +425,91 @@
         norm = lax.fori_loop(0, CG_ITERS - 1, cg, total(resid * resid))
         direction = vec_p[...]
         along = times_rows(scale * direction)
-        bend = small_sum(total(curv[...] * along * along), step, fill + CG_ITERS)
+
+        def hand_out():
+            @pl.when(step == NEWTON - 1)
+            def _():
+                send_rows(along)
+
+        bend = small_sum(total(curv[...] * along * along), step, hand_out)
         size = norm / (bend + ridge_fixed * total(direction * direction))
         score[...] = score[...] + size * along
         vec_w[...] = weights + (vec_u[...] + size * direction)
-        return carry
-
-    lax.fori_loop(0, NEWTON, newton, 0)
+        return size
+
+    def send_rows(along):
+        row_vals[...] = jnp.zeros_like(row_vals)
+        row_vals[0:1, :] = score[...]
+        row_vals[1:2, :] = along
+        row_vals[2:3, :] = target
+        row_vals[3:4, :] = lax.rem(member_ref[...], MEM_DEV).astype(jnp.float32) + 1.0
+        parts = jnp.concatenate([p.astype(jnp.float32) for p in three_parts(row_vals[...])], axis=0)
+        parts = jnp.concatenate([parts, jnp.zeros_like(parts[0:8])], axis=0).astype(jnp.bfloat16)
+        for turn in range(1, n_mem + 1):
+            first = pl.multiple_of(lax.rem(me_mem + turn, n_mem) * cap, cap)
+            got = lax.dot_general(
+                parts, pick[pl.ds(first, cap), :], NT, preferred_element_type=jnp.float32
+            )
+            got = got[0:8] + got[8:16] + got[16:24]
+            if turn < n_mem:
+                w_send[turn - 1] = got
+                pltpu.make_async_remote_copy(
+                    src_ref=w_send.at[turn - 1],
+                    dst_ref=w_recv.at[turn - 1],
+                    send_sem=ws_sem,
+                    recv_sem=wr_sem,
+                    device_id=peer(turn),
+                    device_id_type=MESH_ID,
+                ).start()
+            else:
+                w_recv[n_mem - 1] = got
+
+    size = lax.fori_loop(0, NEWTON, newton, jnp.zeros((1, 1), jnp.float32))
     weight_ref[...] = vec_w[...]
-    prob = 1.0 / (1.0 + jnp.exp(-score[...]))
-    local_id = lax.rem(member_ref[...], MEM_DEV).astype(jnp.float32)
-    row_vals[...] = jnp.zeros_like(row_vals)
-    row_vals[0:1, :] = prob * (1.0 - prob)
-    row_vals[1:2, :] = prob - target
-    row_vals[2:3, :] = local_id
-    parts = jnp.concatenate([p.astype(jnp.float32) for p in three_parts(row_vals[...])], axis=0)
-    parts = jnp.concatenate([parts, jnp.zeros_like(parts[0:8])], axis=0).astype(jnp.bfloat16)
-
-    def small_copy(source, target, turn, sends, recvs):
-        return pltpu.make_async_remote_copy(
-            src_ref=source.at[turn - 1],
-            dst_ref=target.at[turn - 1],
-            send_sem=sends.at[turn - 1],
-            recv_sem=recvs.at[turn - 1],
+    if cap % LANES:
+        for first in range(0, slots, LANES):
+            zt_ref[:, first : first + LANES] = z_ref[first : first + LANES, :].T
+    others = w_recv.at[pl.ds(0, n_mem - 1)]
+    pltpu.make_async_copy(others, others, wr_sem).wait()
+    pltpu.make_async_copy(w_send, w_send, ws_sem).wait()
+    arrived = jnp.concatenate([w_recv[t] for t in range(n_mem)], axis=1)
+    prob = 1.0 / (1.0 + jnp.exp(-(arrived[0:1] + size * arrived[1:2])))
+    coef = fit_members(
+        z_ref, zt_ref, prob * (1.0 - prob), prob - arrived[2:3], arrived[3:4] - 1.0,
+        gram, upper, lower,
+    )
+    coef_ref[...] = coef
+    for turn in range(1, n_mem):
+        pltpu.make_async_remote_copy(
+            src_ref=coef_ref,
+            dst_ref=c_recv.at[me_mem],
+            send_sem=cs_sem,
+            recv_sem=cr_sem,
             device_id=peer(turn),
             device_id_type=MESH_ID,
-        )
-
-    for turn in range(1, n_mem + 1):
-        first = pl.multiple_of(lax.rem(me_mem + turn, n_mem) * cap, cap)
-        got = lax.dot_general(
-            parts, pick[pl.ds(first, cap), :], NT, preferred_element_type=jnp.float32
-        )
-        got = got[0:8] + got[8:16] + got[16:24]
-        if turn < n_mem:
-            w_send[turn - 1] = got
-            small_copy(w_send, w_recv, turn, ws_sem, wr_sem).start()
-        else:
-            w_recv[n_mem - 1] = got
-    for turn in range(1, n_mem):
-        z_copy(turn).wait()
-    for turn in range(1, n_mem + 1):
-        source = lax.rem(me_mem + n_mem - turn, n_mem)
-        block = z_ref[pl.ds(pl.multiple_of(source * cap, cap), cap), :]
-        zt_ref[:, (turn - 1) * cap : turn * cap] = block.T
-        zs_ref[(turn - 1) * cap : turn * cap, :] = block
-    for turn in range(1, n_mem):
-        small_copy(w_send, w_recv, turn, ws_sem, wr_sem).wait()
-    arrived = jnp.concatenate([w_recv[t] for t in range(n_mem)], axis=1)
-    scores = fit_members(
-        zs_ref, zt_ref, arrived[0:1], arrived[1:2], arrived[2:3], coef_ref, gram, upper, lower
+        ).start()
+    c_recv[me_mem] = coef
+    others = c_recv.at[pl.ds(0, n_mem - 1)]
+    pltpu.make_async_copy(others, others, cr_sem).wait()
+    pltpu.make_async_copy(others, others, cs_sem).wait()
+    coefs = jnp.concatenate([c_recv[i] for i in range(n_mem)], axis=0)
+    upper_part = coefs.astype(jnp.bfloat16)
+    lower_part = (coefs - upper_part.astype(jnp.float32)).astype(jnp.bfloat16)
+    got = lax.dot_general(
+        jnp.concatenate([upper_part, lower_part], axis=0), re_ref[...], NT,
+        preferred_element_type=jnp.float32,
     )
-    for turn in range(1, n_mem + 1):
-        back = jnp.broadcast_to(scores[:, (turn - 1) * cap : turn * cap], (8, cap))
-        if turn < n_mem:
-            s_send[n_mem - turn - 1] = back
-        else:
-            s_recv[n_mem - 1] = back
-    for turn in range(1, n_mem):
-        small_copy(s_send, s_recv, turn, ss_sem, sr_sem).start()
-    for turn in range(1, n_mem):
-        small_copy(s_send, s_recv, turn, ss_sem, sr_sem).wait()
-    result = jnp.zeros((1, rows), jnp.float32)
-    for turn in range(1, n_mem + 1):
-        owner = lax.rem(me_mem + n_mem - turn, n_mem)
-        value = s_recv[turn - 1][0:1]
-        p1, p2, p3 = (p.astype(jnp.float32) for p in three_parts(value))
-        at = lax.broadcasted_iota(jnp.int32, (16, cap), 0)
-        stack = jnp.where(at == 0, p1, jnp.where(at == 1, p2, jnp.where(at == 2, p3, 0.0)))
-        got = lax.dot_general(
-            stack.astype(jnp.bfloat16),
-            pick[pl.ds(pl.multiple_of(owner * cap, cap), cap), :],
-            NN,
-            preferred_element_type=jnp.float32,
-        )
-        result = result + (got[0:1] + got[1:2] + got[2:3])
-    offsets_ref[...] = result
+    members = n_mem * MEM_DEV
+    at = lax.broadcasted_iota(jnp.int32, (members, rows), 0)
+    own = at == lax.rem(member_ref[...], members)
+    offsets_ref[...] = jnp.sum(
+        jnp.where(own, got[0:members] + got[members:], 0.0), axis=0, keepdims=True
+    )
+
+
+def hand_over(*refs):
+    for source, target in zip(refs[:3], refs[3:]):
+        target[...] = source[...]
 
 
 def on_device(n_grp, n_mem, features, re_features, member_id, slot, labels, offsets, feature_scale, w_start):
@@ -525,12 +554,10 @@
             pltpu.VMEM((slots, rows), bf16),
             pltpu.VMEM((n_mem - 1, cap, inner), bf16),
             pltpu.VMEM((slots, inner), bf16),
-            pltpu.VMEM((slots, inner), bf16),
             pltpu.VMEM((inner, slots), bf16),
             pltpu.VMEM((n_mem - 1, 8, cap), f32),
             pltpu.VMEM((n_mem, 8, cap), f32),
-            pltpu.VMEM((n_mem - 1, 8, cap), f32),
-            pltpu.VMEM((n_mem, 8, cap), f32),
+            pltpu.VMEM((n_mem, MEM_DEV, inner), f32),
             pltpu.VMEM((MEM_DEV, inner, inner), f32),
             pltpu.VMEM((inner, slots), bf16),
             pltpu.VMEM((inner, slots), bf16),
@@ -545,10 +572,7 @@
             dma((NEWTON,)),
             dma((n_mem - 1,)),
             dma((n_mem - 1,)),
-            dma((n_mem - 1,)),
-            dma((n_mem - 1,)),
-            dma((n_mem - 1,)),
-            dma((n_mem - 1,)),
+            dma, dma, dma, dma,
         ],
         compiler_params=pltpu.CompilerParams(
             collective_id=0, has_side_effects=True, vmem_limit_bytes=60 << 20
@@ -564,6 +588,15 @@
         feature_scale.reshape(lines, LANES),
         w_start.reshape(lines, LANES),
     )
+    weights, member_coef, row_offsets = pl.pallas_call(
+        hand_over,
+        out_shape=tuple(
+            jax.ShapeDtypeStruct(x.shape, x.dtype) for x in (weights, member_coef, row_offsets)
+        ),
+        in_specs=[whole] * 3,
+        out_specs=(whole,) * 3,
+        name="hand_over",
+    )(weights, member_coef, row_offsets)
     return (weights.reshape(-1), member_coef, row_offsets.reshape(-1))
 
 

time: 142 us -> 123 us (0.87)
  Pallas kernels: 137 us -> 122 us
  local copies, waits for them, and re-layouts: 3.89 us -> 0 us
    pallas_call x1, Pallas kernels: 137 us -> 121 us  [on_device(): pl.pallas_call(functools.partial(window_kernel, n_grp, n_mem), out_shape=...]
    unnamed x3 -> x0, local copies, waits for them, and re-layouts: 3.89 us -> none
where the time goes in v2:
time: 123 us
  Pallas kernels  122 us (99%)
    pallas_call x1, Pallas kernels, on_device(): pl.pallas_call(functools.partial(window_kernel, n_grp, n_mem), out_shape=...  121 us

profile of v2, /device:TPU:0, one launch (start us, length us, event | category | flops | bytes accessed | tf_op | source)
XLA Modules:
  0.0 122.5 jit_solution(9073994550082443923)
XLA Ops:
  0.6 120.5 %window.1 = (f32[32,128]{1,0:T(8,128)}, f32[8,256]{1,0:T(8,128)}, f32[1,1024]{1,0:T(1,128)}) custom-call(bf16[1024,4096]{1,0:T(8,128)(2,1)} %feat_hbm.1, bf16[1024,256]{1,0:T(8,128)(2,1)} %re_hbm.1, s32[1,1024]{1,0:T(1,128)} %bitcast.10, s32[1,1024]{1,0:T(1,128)} %bitcast.11, s32[1,1024]{1,0:T(1,128)} %bitcast.12, f32[1,1024]{1,0:T(1,128)} %bitcast.13, ...), custom_call_target="tpu_custom_call" | custom-call | tf_op jit(solution)/shard_map/window/pallas_call | solution.py:529
  121.2 1.4 %hand_over.1 = (f32[32,128]{1,0:T(8,128)}, f32[8,256]{1,0:T(8,128)}, f32[1,1024]{1,0:T(1,128)}) custom-call(f32[32,128]{1,0:T(8,128)} %get-tuple-element.9.refs_0_, f32[8,256]{1,0:T(8,128)} %get-tuple-element.10.refs_1_, f32[1,1024]{1,0:T(1,128)} %get-tuple-element.11.refs_2_), custom_call_target="tpu_custom_call" | custom-call | tf_op jit(solution)/shard_map/hand_over/pallas_call | solution.py:591

commit v3 on v2

--- a/solution.py
+++ b/solution.py
@@ -12,7 +12,7 @@
 CG_ITERS = 3
 LANES = 128
 BLOCK = 32
-BUILD_CALLS = 4
+PARTS = 2
 
 ridge_fixed = 1.0
 ridge_member = 1.0
@@ -22,20 +22,26 @@
 TN = (((0,), (0,)), ((), ()))
 
 
-def pair_rows(row):
-    upper = row.astype(jnp.bfloat16).astype(jnp.float32)
-    lower = (row - upper).astype(jnp.bfloat16).astype(jnp.float32)
-    at = lax.broadcasted_iota(jnp.int32, (16, row.shape[1]), 0)
-    both = jnp.where(at == 0, upper, jnp.where(at == 1, lower, 0.0))
-    return both.astype(jnp.bfloat16)
-
-
 def three_parts(value):
     first = value.astype(jnp.bfloat16)
     rest = value - first.astype(jnp.float32)
     second = rest.astype(jnp.bfloat16)
     third = (rest - second.astype(jnp.float32)).astype(jnp.bfloat16)
     return first, second, third
+
+
+def pair_rows(row):
+    at = lax.broadcasted_iota(jnp.int32, (16, row.shape[1]), 0)
+    both = jnp.zeros((16, row.shape[1]), jnp.float32)
+    for i, part in enumerate(three_parts(row)):
+        both = jnp.where(at == i, part.astype(jnp.float32), both)
+    return both.astype(jnp.bfloat16)
+
+
+def tree_sum(parts):
+    while len(parts) > 1:
+        parts = [parts[i] + parts[i + 1] for i in range(0, len(parts), 2)]
+    return parts[0]
 
 
 def split_six(value, axis, left):
@@ -184,16 +190,18 @@
     n_grp, n_mem,
     feat_hbm, re_hbm, member_hbm, slot_hbm, label_hbm, offset_hbm, scale_hbm, start_hbm,
     weight_ref, coef_ref, offsets_ref,
-    feat, re_ref, member_ref, slot_ref, label_ref, offset_ref, scale_ref, vec_w,
-    vec_u, vec_r, vec_p, curv, score, near_send, near_recv, far_send, far_recv, one_send, one_recv,
+    feat, feat_t, re_ref, member_ref, slot_ref, label_ref, offset_ref, scale_ref, vec_w,
+    vec_u, vec_r, vec_p, curv, score, along_ref, rest_ref, near_send, near_recv, far_send, far_recv, one_send, one_recv,
     pick, z_send, z_ref, zt_ref, w_send, w_recv, c_recv, gram, upper, lower, row_vals,
     load_sem, feat_sem, ns_sem, nr_sem, fs_sem, fr_sem, os_sem, or_sem, zs_sem, zr_sem, ws_sem, wr_sem, cs_sem, cr_sem,
 ):
     rows, width = feat.shape
     lines = width // LANES
+    half = lines // PARTS
     slots = z_ref.shape[0]
     cap = slots // n_mem
-    each = pl.cdiv(n_mem, BUILD_CALLS)
+    each = (n_mem - 1) // (NEWTON * CG_ITERS)
+    early = n_mem - each * NEWTON * CG_ITERS
     direct = n_grp * n_mem <= 32
     me_grp = lax.axis_index("grp")
     me_mem = lax.axis_index("mem")
@@ -214,7 +222,7 @@
         )
         for first in range(0, rows, 256)
     ]
-    for load in loads[:4] + feat_loads + loads[4:]:
+    for load in loads + feat_loads:
         load.start()
 
     low = 2
@@ -241,7 +249,7 @@
     if direct:
         for turn in range(1, n_grp * n_mem):
             pl.semaphore_signal(barrier, inc=1, device_id=any_peer(turn), device_id_type=MESH_ID)
-        pl.semaphore_wait(barrier, n_grp * n_mem - 1)
+        greeted = n_grp * n_mem - 1
     else:
         for turn in range(1, n_mem):
             pl.semaphore_signal(
@@ -249,9 +257,7 @@
             )
         for turn in range(1, near):
             pl.semaphore_signal(barrier, inc=1, device_id=near_peer(turn), device_id_type=MESH_ID)
-        pl.semaphore_wait(barrier, n_mem - 1 + near - 1)
-    for load in loads[:4]:
-        load.wait()
+        greeted = n_mem - 1 + near - 1
 
     def peer(turn):
         return (me_grp, lax.rem(me_mem + turn, n_mem))
@@ -282,149 +288,208 @@
         def _():
             z_ref[(n_mem - 1) * cap :, :] = block
 
-    def exchange(value, call, size, me, peer_of, source, slots_of, sends, recvs, between=None):
-        source[call] = value
+    def begin(value, call, part, size, me, peer_of, source, slots_of, sends, recvs):
+        at = pl.ds(part * half, half)
+        source[call, at] = value
         for turn in range(1, size):
             pltpu.make_async_remote_copy(
-                src_ref=source.at[call],
-                dst_ref=slots_of.at[call, me],
-                send_sem=sends.at[call],
-                recv_sem=recvs.at[call],
+                src_ref=source.at[call, at],
+                dst_ref=slots_of.at[call, me, at],
+                send_sem=sends.at[call, part],
+                recv_sem=recvs.at[call, part],
                 device_id=peer_of(turn),
                 device_id_type=MESH_ID,
             ).start()
-        slots_of[call, me] = value
-        if between is not None:
-            between()
-        others = slots_of.at[call, pl.ds(0, size - 1)]
-        pltpu.make_async_copy(others, others, recvs.at[call]).wait()
-        pltpu.make_async_copy(others, others, sends.at[call]).wait()
-        parts = [slots_of[call, i] for i in range(size)]
-        while len(parts) > 1:
-            parts = [parts[i] + parts[i + 1] for i in range(0, len(parts), 2)]
-        return parts[0]
+        slots_of[call, me, at] = value
+
+    def finish(call, part, size, slots_of, sends, recvs):
+        at = pl.ds(part * half, half)
+        others = slots_of.at[call, pl.ds(0, size - 1), at]
+        pltpu.make_async_copy(others, others, recvs.at[call, part]).wait()
+        pltpu.make_async_copy(others, others, sends.at[call, part]).wait()
+        return tree_sum([slots_of[call, i, at] for i in range(size)])
+
+    def begin_near(value, call, part):
+        begin(value, call, part, near, me_near, near_peer, near_send, near_recv, ns_sem, nr_sem)
+
+    def finish_near(call, part):
+        return finish(call, part, near, near_recv, ns_sem, nr_sem)
+
+    def begin_far(value, call, part):
+        begin(value, call, part, high, me_high, far_peer, far_send, far_recv, fs_sem, fr_sem)
+
+    def finish_far(call, part):
+        return finish(call, part, high, far_recv, fs_sem, fr_sem)
 
     def regroup(call):
         for q in range(each):
-            @pl.when(call * each + q < n_mem)
-            def _():
-                build(call * each + q + 1)
+            build(early + call * each + q + 1)
 
     def forward(call):
         for q in range(each):
-            turn = call * each + q + 1
+            turn = early + call * each + q + 1
 
             @pl.when(turn < n_mem)
             def _():
                 z_copy(turn).start()
 
+    def settle(turn):
+        @pl.when(turn < n_mem)
+        def _():
+            z_copy(turn).wait()
+
+        if cap % LANES == 0:
+            at = pl.ds(pl.multiple_of((turn - 1) * cap, cap), cap)
+            zt_ref[:, at] = z_ref[at, :].T
+
     def turn_over(call):
         for q in range(each):
-            turn = (call - 2) * each + q + 1
-
-            @pl.when((turn >= 1) & (turn < n_mem))
-            def _():
-                z_copy(turn).wait()
-
-            if cap % LANES == 0:
-
-                @pl.when((turn >= 1) & (turn <= n_mem))
-                def _():
-                    at = pl.ds(pl.multiple_of((turn - 1) * cap, cap), cap)
-                    zt_ref[:, at] = z_ref[at, :].T
-
-    def all_sum(value, call, fills=True):
-        value = exchange(
-            value, call, near, me_near, near_peer, near_send, near_recv, ns_sem, nr_sem,
-            functools.partial(regroup, call) if fills else None,
-        )
-        value = exchange(
-            value, call, high, me_high, far_peer, far_send, far_recv, fs_sem, fr_sem,
-            functools.partial(turn_over, call) if fills else None,
-        )
-        if fills:
-            forward(call)
-        return value
+            settle(call * each + q + 1)
+
+        @pl.when(call == NEWTON * CG_ITERS - 1)
+        def _():
+            for q in range(early):
+                settle((call + 1) * each + q + 1)
+
+    def reduce_columns(row, call):
+        pair = pair_rows(row)
+        for part in range(PARTS):
+            begin_near(times_columns(pair, part), call, part)
+        @pl.when(call == 0)
+        def _():
+            transpose_features()
+
+        regroup(call)
+        for part in range(PARTS):
+            begin_far(finish_near(call, part), call, part)
+        turn_over(call)
+        sums, image = [], None
+        for part in range(PARTS):
+            value = scale[part * half : (part + 1) * half] * finish_far(call, part)
+            if part == PARTS - 1:
+                forward(call)
+            got = times_rows(value, part)
+            image = got if image is None else image + got
+            sums.append(value)
+        return jnp.concatenate(sums, axis=0), image
 
     def small_sum(value, call, between):
-        value = jnp.broadcast_to(value, (1, LANES))
         if direct:
-            value = exchange(
-                value, call, n_grp * n_mem, me_all, any_peer, one_send, one_recv, os_sem, or_sem,
-                between,
-            )
-            return value[:, 0:1]
+            value = jnp.broadcast_to(value, (1, LANES))
+            one_send[call] = value
+            for turn in range(1, n_grp * n_mem):
+                pltpu.make_async_remote_copy(
+                    src_ref=one_send.at[call],
+                    dst_ref=one_recv.at[call, me_all],
+                    send_sem=os_sem.at[call],
+                    recv_sem=or_sem.at[call],
+                    device_id=any_peer(turn),
+                    device_id_type=MESH_ID,
+                ).start()
+            one_recv[call, me_all] = value
+            between()
+            others = one_recv.at[call, pl.ds(0, n_grp * n_mem - 1)]
+            pltpu.make_async_copy(others, others, or_sem.at[call]).wait()
+            pltpu.make_async_copy(others, others, os_sem.at[call]).wait()
+            return tree_sum([one_recv[call, i] for i in range(n_grp * n_mem)])[:, 0:1]
         between()
-        wide = jnp.broadcast_to(value, (lines, LANES))
-        return all_sum(wide, NEWTON * CG_ITERS + call, False)[0:1, 0:1]
-
-    def times_rows(vector, loading=False):
-        row = jnp.concatenate([vector[i : i + 1, :] for i in range(lines)], axis=1)
-        pair = pair_rows(row)
+        call = NEWTON * CG_ITERS + call
+        begin_near(jnp.broadcast_to(value, (half, LANES)), call, 0)
+        begin_far(finish_near(call, 0), call, 0)
+        return finish_far(call, 0)[0:1, 0:1]
+
+    def first_rows(vector):
+        pair = pair_rows(jnp.concatenate([vector[i : i + 1, :] for i in range(lines)], axis=1))
         parts = []
         for first in range(0, rows, 256):
-            if loading:
-                feat_loads[first // 256].wait()
+            feat_loads[first // 256].wait()
             got = lax.dot_general(
                 pair, feat[first : first + 256, :], NT, preferred_element_type=jnp.float32
             )
-            parts.append(got[0:1] + got[1:2])
+            parts.append(got[0:1] + got[1:2] + got[2:3])
         return jnp.concatenate(parts, axis=1)
 
-    def times_columns(row):
-        pair = pair_rows(row)
+    def transpose_features():
+        @pl.loop(0, rows // 256)
+        def _(r):
+            at = pl.ds(pl.multiple_of(r * 256, 256), 256)
+            for first in range(0, width, 256):
+                feat_t[first : first + 256, at] = feat[at, first : first + 256].T
+
+    def times_rows(value, part):
+        vector = scale[part * half : (part + 1) * half] * value
+        pair = pair_rows(jnp.concatenate([vector[i : i + 1, :] for i in range(half)], axis=1))
+        at = slice(part * half * LANES, (part + 1) * half * LANES)
         parts = []
-        for first in range(0, width, 256):
+        for first in range(0, rows, 256):
+            got = lax.dot_general(
+                pair, feat_t[at, first : first + 256], NN, preferred_element_type=jnp.float32
+            )
+            parts.append(got[0:1] + got[1:2] + got[2:3])
+        return jnp.concatenate(parts, axis=1)
+
+    def times_columns(pair, part):
+        parts = []
+        for first in range(part * half * LANES, (part + 1) * half * LANES, 256):
             got = lax.dot_general(
                 pair, feat[:, first : first + 256], NN, preferred_element_type=jnp.float32
             )
-            got = got[0:1] + got[1:2]
+            got = got[0:1] + got[1:2] + got[2:3]
             parts += [got[:, at : at + LANES] for at in range(0, 256, LANES)]
         return jnp.concatenate(parts, axis=0)
 
     def total(value):
         return jnp.sum(jnp.sum(value, axis=1, keepdims=True), axis=0, keepdims=True)
 
+    for load in loads:
+        load.wait()
     scale = scale_ref[...]
     target = label_ref[...].astype(jnp.float32)
 
-    score[...] = times_rows(scale * vec_w[...], True)
+    for turn in range(1, early + 1):
+        build(turn)
+    pl.semaphore_wait(barrier, greeted)
+    for turn in range(1, early + 1):
+        z_copy(turn).start()
+    score[...] = first_rows(scale * vec_w[...])
 
     def newton(step, carry):
         weights = vec_w[...]
         margin = score[...] + offset_ref[...]
         prob = 1.0 / (1.0 + jnp.exp(-margin))
         curv[...] = prob * (1.0 - prob)
-        grad = times_columns(prob - target)
-
-        @pl.when(step == 0)
-        def _():
-            for load in loads[4:]:
-                load.wait()
 
         base = step * CG_ITERS
-        resid = -(scale * all_sum(grad, base) + ridge_fixed * weights)
+        summed, along = reduce_columns(prob - target, base)
+        resid = -(summed + ridge_fixed * weights)
+        along = -(along + ridge_fixed * score[...])
         vec_r[...] = resid
         vec_p[...] = resid
         vec_u[...] = jnp.zeros_like(resid)
+        rest_ref[...] = along
+        along_ref[...] = along
 
         def cg(k, norm):
             direction = vec_p[...]
-            along = times_rows(scale * direction)
-            image = all_sum(times_columns(curv[...] * along), base + 1 + k)
-            image = scale * image + ridge_fixed * direction
+            along = along_ref[...]
+            image, seen = reduce_columns(curv[...] * along, base + 1 + k)
+            image = image + ridge_fixed * direction
             size = norm / total(direction * image)
             vec_u[...] = vec_u[...] + size * direction
             score[...] = score[...] + size * along
             left = vec_r[...] - size * image
             vec_r[...] = left
+            rest = rest_ref[...] - size * (seen + ridge_fixed * along)
+            rest_ref[...] = rest
             new_norm = total(left * left)
-            vec_p[...] = left + new_norm / norm * direction
+            turned = new_norm / norm
+            vec_p[...] = left + turned * direction
+            along_ref[...] = rest + turned * along
             return new_norm
 
         norm = lax.fori_loop(0, CG_ITERS - 1, cg, total(resid * resid))
         direction = vec_p[...]
-        along = times_rows(scale * direction)
+        along = along_ref[...]
 
         def hand_out():
             @pl.when(step == NEWTON - 1)
@@ -537,12 +602,15 @@
         out_specs=(whole,) * 3,
         scratch_shapes=[
             pltpu.VMEM((rows, width), bf16),
+            pltpu.VMEM((width, rows), bf16),
             pltpu.VMEM((rows, inner), bf16),
             pltpu.VMEM((1, rows), i32),
             pltpu.VMEM((1, rows), i32),
             pltpu.VMEM((1, rows), i32),
             pltpu.VMEM((1, rows), f32),
             held, held, held, held, held,
+            pltpu.VMEM((1, rows), f32),
+            pltpu.VMEM((1, rows), f32),
             pltpu.VMEM((1, rows), f32),
             pltpu.VMEM((1, rows), f32),
             pltpu.VMEM((calls, lines, LANES), f32),
@@ -564,10 +632,10 @@
             pltpu.VMEM((8, rows), f32),
             dma((7,)),
             dma((rows // 256,)),
-            dma((calls,)),
-            dma((calls,)),
-            dma((calls,)),
-            dma((calls,)),
+            dma((calls, PARTS)),
+            dma((calls, PARTS)),
+            dma((calls, PARTS)),
+            dma((calls, PARTS)),
             dma((NEWTON,)),
             dma((NEWTON,)),
             dma((n_mem - 1,)),

time: 123 us -> 114 us (0.927)
  Pallas kernels: 122 us -> 113 us
    pallas_call x1, Pallas kernels: 121 us -> 111 us  [on_device(): pl.pallas_call(functools.partial(window_kernel, n_grp, n_mem), out_shape=...]
where the time goes in v3:
time: 114 us; the launch traced here: 113 us
  Pallas kernels  113 us (99%)
    pallas_call x1, Pallas kernels, on_device(): pl.pallas_call(functools.partial(window_kernel, n_grp, n_mem), out_shape=...  111 us

profile of v3, /device:TPU:0, one launch (start us, length us, event | category | flops | bytes accessed | tf_op | source)
XLA Modules:
  0.0 113.4 jit_solution(8931788876830994687)
XLA Ops:
  0.6 111.4 %window.1 = (f32[32,128]{1,0:T(8,128)}, f32[8,256]{1,0:T(8,128)}, f32[1,1024]{1,0:T(1,128)}) custom-call(bf16[1024,4096]{1,0:T(8,128)(2,1)} %feat_hbm.1, bf16[1024,256]{1,0:T(8,128)(2,1)} %re_hbm.1, s32[1,1024]{1,0:T(1,128)} %bitcast.10, s32[1,1024]{1,0:T(1,128)} %bitcast.11, s32[1,1024]{1,0:T(1,128)} %bitcast.12, f32[1,1024]{1,0:T(1,128)} %bitcast.13, ...), custom_call_target="tpu_custom_call" | custom-call | tf_op jit(solution)/shard_map/window/pallas_call | solution.py:594
  112.0 1.4 %hand_over.1 = (f32[32,128]{1,0:T(8,128)}, f32[8,256]{1,0:T(8,128)}, f32[1,1024]{1,0:T(1,128)}) custom-call(f32[32,128]{1,0:T(8,128)} %get-tuple-element.9.refs_0_, f32[8,256]{1,0:T(8,128)} %get-tuple-element.10.refs_1_, f32[1,1024]{1,0:T(1,128)} %get-tuple-element.11.refs_2_), custom_call_target="tpu_custom_call" | custom-call | tf_op jit(solution)/shard_map/hand_over/pallas_call | solution.py:659

commit v4 on v3

--- a/solution.py
+++ b/solution.py
@@ -13,6 +13,7 @@
 LANES = 128
 BLOCK = 32
 PARTS = 2
+ORDER = (4, 3, 5, 2, 7, 6, 1, 8)
 
 ridge_fixed = 1.0
 ridge_member = 1.0
@@ -60,67 +61,100 @@
     def column(value, k):
         return jnp.take_along_axis(value, base + k, axis=1)
 
-    blocks = [(value, column(value, 0), column(value, 1)) for value in blocks]
+    def spread(value, k):
+        return jnp.broadcast_to(value[k : k + 1, :], (8, LANES))
+
+    def tall(value):
+        return jnp.concatenate([value] * (BLOCK // 8), axis=0)
+
+    def start(value):
+        left, right = column(value, 0), column(value, 1)
+        corner = [spread(col, k) for k in (0, 1) for col in (left, right)]
+        return value, left, right, corner
+
+    blocks = [start(value) for value in blocks]
     for k in range(0, BLOCK, 2):
         one, two = place == k, place == k + 1
-        at_one, at_two = one[0:1, :], two[0:1, :]
+        at_one, at_two = one[0:8, :], two[0:8, :]
+        more = k + 2 < BLOCK
         new = []
-        for value, left, right in blocks:
-            ahead = [column(value, k + 2), column(value, k + 3)] if k + 2 < BLOCK else []
-            a, b = left[k : k + 1, :], right[k : k + 1, :]
-            c, d = left[k + 1 : k + 2, :], right[k + 1 : k + 2, :]
+        for value, left, right, (a, b, c, d) in blocks:
+            ahead = [column(value, k + 2), column(value, k + 3)] if more else []
             inverse = 1.0 / (a * d - b * c)
             a, b, c, d = d * inverse, -b * inverse, -c * inverse, a * inverse
 
             def update(value, first, second):
+                first, second = tall(first), tall(second)
                 value = value - left * first - right * second
                 return jnp.where(sub == k, first, jnp.where(sub == k + 1, second, value))
 
-            following = []
-            for col in ahead:
-                top, low = col[k : k + 1, :], col[k + 1 : k + 2, :]
-                following.append(update(col, a * top + b * low, c * top + d * low))
-            top, low = value[k : k + 1, :], value[k + 1 : k + 2, :]
+            firsts = [a * spread(col, k) + b * spread(col, k + 1) for col in ahead]
+            seconds = [c * spread(col, k) + d * spread(col, k + 1) for col in ahead]
+            corner = [
+                spread(col, at) - spread(left, at) * first - spread(right, at) * second
+                for at in ((k + 2, k + 3) if more else ())
+                for col, first, second in zip(ahead, firsts, seconds)
+            ]
+            following = [
+                update(col, first, second) for col, first, second in zip(ahead, firsts, seconds)
+            ]
+            top, low = spread(value, k), spread(value, k + 1)
             first = jnp.where(at_one, a, jnp.where(at_two, b, a * top + b * low))
             second = jnp.where(at_one, c, jnp.where(at_two, d, c * top + d * low))
             value = update(jnp.where(one | two, 0.0, value), first, second)
-            new.append((value, *(following or (left, right))))
+            new.append((value, *(following or (left, right)), corner or (a, b, c, d)))
         blocks = new
-        yield [value for value, _, _ in blocks]
-
-
-def fit_members(z_ref, zt_ref, curv_row, resid_row, local, gram, upper, lower):
+        yield [value for value, *_ in blocks]
+
+
+def fit_members(z_ref, zt_ref, curv_row, resid_row, local, gram, upper, lower, mixed):
     width = z_ref.shape[1]
     slots = z_ref.shape[0]
     count = MEM_DEV
     per = LANES // BLOCK
     blocks = width // BLOCK
-    weighted = zt_ref[...].astype(jnp.float32) * curv_row
+    side = width // 2
+    column = jnp.broadcast_to(curv_row, (LANES, slots)).T
+    column = jnp.concatenate([column] * (width // LANES), axis=1)
+    weighted = z_ref[...].astype(jnp.float32) * column
     first = weighted.astype(jnp.bfloat16)
+    second = (weighted - first.astype(jnp.float32)).astype(jnp.bfloat16)
     upper[...] = first
-    lower[...] = (weighted - first.astype(jnp.float32)).astype(jnp.bfloat16)
+    lower[...] = second
+    mixed[:, 0:side] = first[:, side:]
+    mixed[:, side:] = second[:, side:]
     eye = (
         lax.broadcasted_iota(jnp.int32, (width, width), 0)
         == lax.broadcasted_iota(jnp.int32, (width, width), 1)
     ).astype(jnp.float32)
 
-    @pl.loop(0, count)
+    @pl.loop(0, count, step=2)
     def _(m):
-        mask = jnp.where(local == m.astype(jnp.float32), 1.0, 0.0).astype(jnp.bfloat16)
-        total = lax.dot_general(
-            upper[...] * mask, z_ref[...], NN, preferred_element_type=jnp.float32
-        ) + lax.dot_general(
-            lower[...] * mask, z_ref[...], NN, preferred_element_type=jnp.float32
-        )
-        gram[m] = total + ridge_member * eye
+        masks = [
+            jnp.where(local == (m + i).astype(jnp.float32), 1.0, 0.0).astype(jnp.bfloat16)
+            for i in range(2)
+        ]
+        top = jnp.concatenate([zt_ref[0:side, :] * mask for mask in masks], axis=0)
+        low = jnp.concatenate([zt_ref[side:, :] * mask for mask in masks], axis=0)
+        top = lax.dot_general(
+            top, upper[...], NN, preferred_element_type=jnp.float32
+        ) + lax.dot_general(top, lower[...], NN, preferred_element_type=jnp.float32)
+        low = lax.dot_general(low, mixed[...], NN, preferred_element_type=jnp.float32)
+        low = low[:, 0:side] + low[:, side:]
+        for i in range(2):
+            at = slice(i * side, (i + 1) * side)
+            gram[m + i, 0:side, :] = top[at] + ridge_member * eye[0:side]
+            gram[m + i, side:, 0:side] = jnp.zeros((side, side), jnp.float32)
+            gram[m + i, side:, side:] = low[at] + ridge_member * eye[side:, side:]
 
     member = lax.broadcasted_iota(jnp.int32, (count, slots), 0).astype(jnp.float32)
     masked = jnp.where(member == local, resid_row, 0.0)
     high = masked.astype(jnp.bfloat16)
     low = (masked - high.astype(jnp.float32)).astype(jnp.bfloat16)
     goal = lax.dot_general(
-        high, z_ref[...], NN, preferred_element_type=jnp.float32
-    ) + lax.dot_general(low, z_ref[...], NN, preferred_element_type=jnp.float32)
+        jnp.concatenate([high, low], axis=0), z_ref[...], NN, preferred_element_type=jnp.float32
+    )
+    goal = goal[0:count] + goal[count:]
 
     place = lax.broadcasted_iota(jnp.int32, (1, width), 1)
     turn = lax.broadcasted_iota(jnp.int32, (count, width), 0)
@@ -192,7 +226,7 @@
     weight_ref, coef_ref, offsets_ref,
     feat, feat_t, re_ref, member_ref, slot_ref, label_ref, offset_ref, scale_ref, vec_w,
     vec_u, vec_r, vec_p, curv, score, along_ref, rest_ref, near_send, near_recv, far_send, far_recv, one_send, one_recv,
-    pick, z_send, z_ref, zt_ref, w_send, w_recv, c_recv, gram, upper, lower, row_vals,
+    pick, z_send, z_ref, zt_ref, w_send, w_recv, c_recv, gram, upper, lower, mixed, row_vals,
     load_sem, feat_sem, ns_sem, nr_sem, fs_sem, fr_sem, os_sem, or_sem, zs_sem, zr_sem, ws_sem, wr_sem, cs_sem, cr_sem,
 ):
     rows, width = feat.shape
@@ -321,13 +355,23 @@
     def finish_far(call, part):
         return finish(call, part, high, far_recv, fs_sem, fr_sem)
 
+    def turn_of(place):
+        if n_mem != len(ORDER):
+            return place + 1
+        if isinstance(place, int):
+            return ORDER[place]
+        turn = jnp.int32(ORDER[0])
+        for i, value in enumerate(ORDER):
+            turn = jnp.where(place == i, jnp.int32(value), turn)
+        return turn
+
     def regroup(call):
         for q in range(each):
-            build(early + call * each + q + 1)
+            build(turn_of(early + call * each + q))
 
     def forward(call):
         for q in range(each):
-            turn = early + call * each + q + 1
+            turn = turn_of(early + call * each + q)
 
             @pl.when(turn < n_mem)
             def _():
@@ -344,12 +388,12 @@
 
     def turn_over(call):
         for q in range(each):
-            settle(call * each + q + 1)
+            settle(turn_of(call * each + q))
 
         @pl.when(call == NEWTON * CG_ITERS - 1)
         def _():
             for q in range(early):
-                settle((call + 1) * each + q + 1)
+                settle(turn_of((call + 1) * each + q))
 
     def reduce_columns(row, call):
         pair = pair_rows(row)
@@ -446,11 +490,11 @@
     scale = scale_ref[...]
     target = label_ref[...].astype(jnp.float32)
 
-    for turn in range(1, early + 1):
-        build(turn)
+    for place in range(early):
+        build(turn_of(place))
     pl.semaphore_wait(barrier, greeted)
-    for turn in range(1, early + 1):
-        z_copy(turn).start()
+    for place in range(early):
+        z_copy(turn_of(place)).start()
     score[...] = first_rows(scale * vec_w[...])
 
     def newton(step, carry):
@@ -541,7 +585,7 @@
     prob = 1.0 / (1.0 + jnp.exp(-(arrived[0:1] + size * arrived[1:2])))
     coef = fit_members(
         z_ref, zt_ref, prob * (1.0 - prob), prob - arrived[2:3], arrived[3:4] - 1.0,
-        gram, upper, lower,
+        gram, upper, lower, mixed,
     )
     coef_ref[...] = coef
     for turn in range(1, n_mem):
@@ -627,8 +671,9 @@
             pltpu.VMEM((n_mem, 8, cap), f32),
             pltpu.VMEM((n_mem, MEM_DEV, inner), f32),
             pltpu.VMEM((MEM_DEV, inner, inner), f32),
-            pltpu.VMEM((inner, slots), bf16),
-            pltpu.VMEM((inner, slots), bf16),
+            pltpu.VMEM((slots, inner), bf16),
+            pltpu.VMEM((slots, inner), bf16),
+            pltpu.VMEM((slots, inner), bf16),
             pltpu.VMEM((8, rows), f32),
             dma((7,)),
             dma((rows // 256,)),

time: 114 us -> 109 us (0.956)
  Pallas kernels: 113 us -> 108 us
    pallas_call x1, Pallas kernels: 111 us -> 107 us  [on_device(): pl.pallas_call(functools.partial(window_kernel, n_grp, n_mem), out_shape=...]
where the time goes in v4:
time: 109 us
  Pallas kernels  108 us (99%)
    pallas_call x1, Pallas kernels, on_device(): pl.pallas_call(functools.partial(window_kernel, n_grp, n_mem), out_shape=...  107 us

profile of v4, /device:TPU:0, one launch (start us, length us, event | category | flops | bytes accessed | tf_op | source)
XLA Modules:
  0.0 109.1 jit_solution(496283431990232602)
XLA Ops:
  0.6 107.1 %window.1 = (f32[32,128]{1,0:T(8,128)}, f32[8,256]{1,0:T(8,128)}, f32[1,1024]{1,0:T(1,128)}) custom-call(bf16[1024,4096]{1,0:T(8,128)(2,1)} %feat_hbm.1, bf16[1024,256]{1,0:T(8,128)(2,1)} %re_hbm.1, s32[1,1024]{1,0:T(1,128)} %bitcast.10, s32[1,1024]{1,0:T(1,128)} %bitcast.11, s32[1,1024]{1,0:T(1,128)} %bitcast.12, f32[1,1024]{1,0:T(1,128)} %bitcast.13, ...), custom_call_target="tpu_custom_call" | custom-call | tf_op jit(solution)/shard_map/window/pallas_call | solution.py:638
  107.8 1.4 %hand_over.1 = (f32[32,128]{1,0:T(8,128)}, f32[8,256]{1,0:T(8,128)}, f32[1,1024]{1,0:T(1,128)}) custom-call(f32[32,128]{1,0:T(8,128)} %get-tuple-element.9.refs_0_, f32[8,256]{1,0:T(8,128)} %get-tuple-element.10.refs_1_, f32[1,1024]{1,0:T(1,128)} %get-tuple-element.11.refs_2_), custom_call_target="tpu_custom_call" | custom-call | tf_op jit(solution)/shard_map/hand_over/pallas_call | solution.py:704

commit v5 on v4

--- a/solution.py
+++ b/solution.py
@@ -197,7 +197,8 @@
                 preferred_element_type=jnp.float32,
             )
             panels += [got[i * BLOCK : (i + 1) * BLOCK, :] for i in range(per)]
-        heads = split_six(goal[:, lo:hi], 1, True)
+        heads = split_six(goal[:, lo:hi], 1, True).astype(jnp.float32)
+        heads = jnp.concatenate([heads, jnp.zeros_like(heads)], axis=0).astype(jnp.bfloat16)
         goal = jnp.where(inside, 0.0, goal)
         following = []
         for m in range(count):
@@ -205,16 +206,22 @@
             if hi < width:
                 left = split_six(rows_now[m][:, hi:], 0, True)
                 update = lax.dot_general(
-                    left[:, 0:BLOCK], right, TN, preferred_element_type=jnp.float32
+                    jnp.concatenate([left[:, 0:BLOCK].T, heads], axis=0), right, NN,
+                    preferred_element_type=jnp.float32,
                 )
-                following.append(jnp.where(inside, 0.0, gram[m, hi : hi + BLOCK, :]) - update)
+                following.append(
+                    jnp.where(inside, 0.0, gram[m, hi : hi + BLOCK, :]) - update[0:BLOCK]
+                )
+                update = update[BLOCK : BLOCK + count]
                 if hi + BLOCK < width:
                     later.append(
                         functools.partial(
                             trailing, m, hi + BLOCK, inside, left[:, BLOCK:], right
                         )
                     )
-            update = lax.dot_general(heads, right, NN, preferred_element_type=jnp.float32)
+            else:
+                update = lax.dot_general(heads, right, NN, preferred_element_type=jnp.float32)
+                update = update[0:count]
             goal = goal - jnp.where(turn == m, update, 0.0)
         rows_now = following
     return -goal
@@ -406,12 +413,11 @@
         regroup(call)
         for part in range(PARTS):
             begin_far(finish_near(call, part), call, part)
+        forward(call)
         turn_over(call)
         sums, image = [], None
         for part in range(PARTS):
             value = scale[part * half : (part + 1) * half] * finish_far(call, part)
-            if part == PARTS - 1:
-                forward(call)
             got = times_rows(value, part)
             image = got if image is None else image + got
             sums.append(value)

time: 109 us -> 108 us (level)
    pallas_call x1, Pallas kernels: 107 us -> 106 us  [on_device(): pl.pallas_call(functools.partial(window_kernel, n_grp, n_mem), out_shape=...]
where the time goes in v5:
time: 108 us; the launch traced here: 107 us
  Pallas kernels  107 us (99%)
    pallas_call x1, Pallas kernels, on_device(): pl.pallas_call(functools.partial(window_kernel, n_grp, n_mem), out_shape=...  106 us

profile of v5, /device:TPU:0, one launch (start us, length us, event | category | flops | bytes accessed | tf_op | source)
XLA Modules:
  0.0 107.5 jit_solution(4010579619543505538)
XLA Ops:
  0.6 105.5 %window.1 = (f32[32,128]{1,0:T(8,128)}, f32[8,256]{1,0:T(8,128)}, f32[1,1024]{1,0:T(1,128)}) custom-call(bf16[1024,4096]{1,0:T(8,128)(2,1)} %feat_hbm.1, bf16[1024,256]{1,0:T(8,128)(2,1)} %re_hbm.1, s32[1,1024]{1,0:T(1,128)} %bitcast.10, s32[1,1024]{1,0:T(1,128)} %bitcast.11, s32[1,1024]{1,0:T(1,128)} %bitcast.12, f32[1,1024]{1,0:T(1,128)} %bitcast.13, ...), custom_call_target="tpu_custom_call" | custom-call | tf_op jit(solution)/shard_map/window/pallas_call | solution.py:644
  106.1 1.4 %hand_over.1 = (f32[32,128]{1,0:T(8,128)}, f32[8,256]{1,0:T(8,128)}, f32[1,1024]{1,0:T(1,128)}) custom-call(f32[32,128]{1,0:T(8,128)} %get-tuple-element.9.refs_0_, f32[8,256]{1,0:T(8,128)} %get-tuple-element.10.refs_1_, f32[1,1024]{1,0:T(1,128)} %get-tuple-element.11.refs_2_), custom_call_target="tpu_custom_call" | custom-call | tf_op jit(solution)/shard_map/hand_over/pallas_call | solution.py:710

commit v6 on v5

--- a/solution.py
+++ b/solution.py
@@ -13,7 +13,7 @@
 LANES = 128
 BLOCK = 32
 PARTS = 2
-ORDER = (4, 3, 5, 2, 7, 6, 1, 8)
+ORDER = (3, 5, 4, 2, 7, 6, 1, 8)
 
 ridge_fixed = 1.0
 ridge_member = 1.0

time: 108 us -> 107 us (level)
  no operation moved by 1% of the time
where the time goes in v6:
time: 107 us
  Pallas kernels  107 us (100%)
    pallas_call x1, Pallas kernels, on_device(): pl.pallas_call(functools.partial(window_kernel, n_grp, n_mem), out_shape=...  105 us

profile of v6, /device:TPU:0, one launch (start us, length us, event | category | flops | bytes accessed | tf_op | source)
XLA Modules:
  0.0 107.2 jit_solution(12643160172111659098)
XLA Ops:
  0.6 105.2 %window.1 = (f32[32,128]{1,0:T(8,128)}, f32[8,256]{1,0:T(8,128)}, f32[1,1024]{1,0:T(1,128)}) custom-call(bf16[1024,4096]{1,0:T(8,128)(2,1)} %feat_hbm.1, bf16[1024,256]{1,0:T(8,128)(2,1)} %re_hbm.1, s32[1,1024]{1,0:T(1,128)} %bitcast.10, s32[1,1024]{1,0:T(1,128)} %bitcast.11, s32[1,1024]{1,0:T(1,128)} %bitcast.12, f32[1,1024]{1,0:T(1,128)} %bitcast.13, ...), custom_call_target="tpu_custom_call" | custom-call | tf_op jit(solution)/shard_map/window/pallas_call | solution.py:644
  105.9 1.4 %hand_over.1 = (f32[32,128]{1,0:T(8,128)}, f32[8,256]{1,0:T(8,128)}, f32[1,1024]{1,0:T(1,128)}) custom-call(f32[32,128]{1,0:T(8,128)} %get-tuple-element.9.refs_0_, f32[8,256]{1,0:T(8,128)} %get-tuple-element.10.refs_1_, f32[1,1024]{1,0:T(1,128)} %get-tuple-element.11.refs_2_), custom_call_target="tpu_custom_call" | custom-call | tf_op jit(solution)/shard_map/hand_over/pallas_call | solution.py:710
